TPU v7x, 256 devices: a whole 4x4x8 slice. The times are simulated.
256 devices in a mesh: slab: 64 (over x, z, core), geo: 4 (over y).
Axes of the slice: x: 4, y: 4, z: 8, core: 2. Of those that a mesh axis runs over, the one named last changes fastest.
Arguments:
- enc_feat: float32 [32768, 32, 128], P(('geo', 'slab')), parts along dimension 0, may hold values from -6 to 6
- enc_pos: float32 [32768, 3, 128], P(('geo', 'slab')), parts along dimension 0, may hold values from -1 to 1
- enc_dest: int32 [32768, 1], P(('geo', 'slab')), parts along dimension 0, may hold values from 0 to 63; in each aligned block of 128 rows (0 to 127, 128 to 255, ...) at most 6 rows name the same one
- enc_line: int32 [32768], P(('geo', 'slab')), parts along dimension 0, may hold values from 0 to 255
- dec_pos: float32 [32768, 3, 128], P(('geo', 'slab')), parts along dimension 0, may hold values from -1 to 1
- dec_dest: int32 [32768, 1], P(('geo', 'slab')), parts along dimension 0, may hold values from 0 to 63; in each aligned block of 128 rows (0 to 127, 128 to 255, ...) at most 6 rows name the same one
- dec_line: int32 [32768], P(('geo', 'slab')), parts along dimension 0, may hold values from 0 to 255
- mode_weight: bfloat16 [64, 64, 33, 2048], P(None, 'slab'), may hold values from -3 to 3
- skip_weight: float32 [32, 32], replicated, may hold values from -1 to 1
- skip_bias: float32 [32], replicated, may hold values from -3 to 3
- dec_weight: float32 [32, 32], replicated, may hold values from -1 to 1
- out_weight: float32 [32], replicated, may hold values from -1 to 1
Outputs:
- pressure: float32 [32768, 128], P(('geo', 'slab')), parts along dimension 0
There are 4 independent parts, one for each index of `geo`. A program takes and returns all parts, laid end to end along the dimension named above; an argument that names none is the same for every part. Nothing has to cross between parts.
Inputs may be any that keep to these rules, and one draw needn't show every extreme that they name: `enc_dest`: among the blocks of one device each slab number appears at most 6 times; some device names some slab exactly 6 times. `dec_dest`: among the blocks of one device each slab number appears at most 6 times; some device names some slab exactly 6 times.
All inputs are finite; a program needn't handle non-finite values.
Results may differ from a plain program's by a relative error of at most 0.0003.
Values sent between devices are 32-bit elements; how exact they have to be, the bound alone decides.
A program may use at most 128 MiB of HBM per device.

v0:
```python
import math

import jax
import jax.numpy as jnp
from jax import lax
from jax.sharding import PartitionSpec as P

NX = 128
NY = 128
NZ = 128
MX = 64
MY = 64
MZ = 33


radius_scale = 0.7
spread_cells = 1.5


def kernel_rows(positions):
    planar = positions[:, 0, :] ** 2 + positions[:, 1, :] ** 2
    radial = jnp.exp(-planar / (2.0 * radius_scale**2))
    height = (positions[:, 2, :] + 1.0) * (0.5 * (NZ - 1))
    grid_cells = jnp.arange(NZ, dtype=jnp.float32)
    offset = grid_cells[None, None, :] - height[:, :, None]
    return radial[:, :, None] * jnp.exp(-offset * offset / (2.0 * spread_cells**2))


def kept_freq(length, kept_count):
    counter = jnp.arange(kept_count, dtype=jnp.int32)
    return jnp.where(counter < kept_count // 2, counter, counter + length - kept_count)


def phase_table(length, frequency):
    grid_cells = jnp.arange(length, dtype=jnp.int32)
    phase_turns = grid_cells[:, None] * frequency[None, :] % length
    angles = phase_turns.astype(jnp.float32) * (2.0 * math.pi / length)
    return (jnp.cos(angles), jnp.sin(angles))


def decode_blocks(line_data, positions, dec_weight, out_weight):
    kernel = kernel_rows(positions)
    nearby = jnp.einsum("bcz,bpz->bcp", line_data, kernel, precision=lax.Precision.HIGHEST)
    hidden_act = jax.nn.gelu(
        jnp.einsum("bcp,cd->bdp", nearby, dec_weight, precision=lax.Precision.HIGHEST)
    )
    return jnp.einsum("bdp,d->bp", hidden_act, out_weight, precision=lax.Precision.HIGHEST)


def slot_rows(owners, slab_count, capacity):
    onehot = (owners[:, None] == jnp.arange(slab_count, dtype=jnp.int32)[None, :]).astype(jnp.int32)
    before = jnp.cumsum(onehot, axis=0) - onehot
    slot_number = jnp.sum(before * onehot, axis=1)
    return owners * capacity + slot_number


def find_source(slot_index, slot_total):
    matches = (slot_index[None, :] == jnp.arange(slot_total, dtype=jnp.int32)[:, None]).astype(
        jnp.int32
    )
    filled = jnp.sum(matches, axis=1) > 0
    counter = jnp.arange(slot_index.shape[0], dtype=jnp.int32)
    source_block = jnp.sum(matches * counter[None, :], axis=1)
    return (source_block, filled)


def einsum_exact(form, left, right):
    return jnp.einsum(form, left, right, precision=lax.Precision.HIGHEST)


def local(
    enc_feat,
    enc_pos,
    enc_dest,
    enc_line,
    dec_pos,
    dec_dest,
    dec_line,
    mode_weight,
    skip_weight,
    skip_bias,
    dec_weight,
    out_weight,
):
    slab_count = lax.axis_size("slab")
    blocks, channels, points = enc_feat.shape
    capacity = max(2, 3 * blocks // slab_count)
    slot_total = slab_count * capacity
    planes = NX // slab_count
    lines_dev = planes * NY
    slot_index = slot_rows(enc_dest[:, 0], slab_count, capacity)
    source_block, filled = find_source(slot_index, slot_total)
    line_ids = jnp.where(filled, enc_line[source_block], -1)
    terms = einsum_exact("bcp,bpz->bcz", enc_feat, kernel_rows(enc_pos))
    packed = jnp.where(filled[:, None, None], terms[source_block], 0.0)
    got_terms, got_lines = (
        lax.all_to_all(packed, "slab", split_axis=0, concat_axis=0, tiled=True),
        lax.all_to_all(line_ids, "slab", split_axis=0, concat_axis=0, tiled=True),
    )
    target = jnp.where(got_lines >= 0, got_lines, lines_dev)
    latent = jax.ops.segment_sum(got_terms, target, num_segments=lines_dev + 1)[:lines_dev]
    latent_field = latent.reshape(planes, NY, channels, NZ)
    z_cos, z_sin = phase_table(NZ, jnp.arange(MZ, dtype=jnp.int32))
    y_cos, y_sin = phase_table(NY, kept_freq(NY, MY))
    x_cos, x_sin = phase_table(NX, kept_freq(NX, MX))
    z_real = einsum_exact("xycn,nk->xyck", latent_field, z_cos)
    z_imag = -einsum_exact("xycn,nk->xyck", latent_field, z_sin)
    y_real = einsum_exact("xnck,nj->xjck", z_real, y_cos) + einsum_exact(
        "xnck,nj->xjck", z_imag, y_sin
    )
    y_imag = einsum_exact("xnck,nj->xjck", z_imag, y_cos) - einsum_exact(
        "xnck,nj->xjck", z_real, y_sin
    )
    stacked = jnp.stack([y_real, y_imag], axis=2).reshape(planes, MY, 2 * channels * MZ)
    spectrum = lax.all_to_all(stacked, "slab", split_axis=1, concat_axis=0, tiled=True)
    mode_share = spectrum.shape[1]
    spectrum = spectrum.reshape(NX, mode_share, 2, channels, MZ)
    m_real = spectrum[:, :, 0]
    m_imag = spectrum[:, :, 1]
    s_real = einsum_exact("nbck,nj->jbck", m_real, x_cos) + einsum_exact(
        "nbck,nj->jbck", m_imag, x_sin
    )
    s_imag = einsum_exact("nbck,nj->jbck", m_imag, x_cos) - einsum_exact(
        "nbck,nj->jbck", m_real, x_sin
    )
    weights = mode_weight.astype(jnp.float32).reshape(MX, mode_share, MZ, 2, channels, channels)
    w_real = weights[:, :, :, 0]
    w_imag = weights[:, :, :, 1]
    o_real = einsum_exact("abck,abkcd->abdk", s_real, w_real) - einsum_exact(
        "abck,abkcd->abdk", s_imag, w_imag
    )
    o_imag = einsum_exact("abck,abkcd->abdk", s_real, w_imag) + einsum_exact(
        "abck,abkcd->abdk", s_imag, w_real
    )
    back_real = (
        einsum_exact("jbdk,nj->nbdk", o_real, x_cos) - einsum_exact("jbdk,nj->nbdk", o_imag, x_sin)
    ) / NX
    back_imag = (
        einsum_exact("jbdk,nj->nbdk", o_real, x_sin) + einsum_exact("jbdk,nj->nbdk", o_imag, x_cos)
    ) / NX
    inverse = jnp.stack([back_real, back_imag], axis=2).reshape(NX, mode_share, 2 * channels * MZ)
    planar = lax.all_to_all(inverse, "slab", split_axis=0, concat_axis=1, tiled=True)
    planar = planar.reshape(planes, MY, 2, channels, MZ)
    p_real = planar[:, :, 0]
    p_imag = planar[:, :, 1]
    q_real = (
        einsum_exact("xjck,nj->xnck", p_real, y_cos) - einsum_exact("xjck,nj->xnck", p_imag, y_sin)
    ) / NY
    q_imag = (
        einsum_exact("xjck,nj->xnck", p_real, y_sin) + einsum_exact("xjck,nj->xnck", p_imag, y_cos)
    ) / NY
    z_weight = jnp.where(jnp.arange(MZ, dtype=jnp.int32) == 0, 1.0, 2.0).astype(jnp.float32) / NZ
    spectral = einsum_exact("xyck,nk->xycn", q_real, z_cos * z_weight[None, :]) - einsum_exact(
        "xyck,nk->xycn", q_imag, z_sin * z_weight[None, :]
    )
    skip_term = einsum_exact("xycn,cd->xydn", latent_field, skip_weight)
    hidden = jax.nn.gelu(spectral + skip_term + skip_bias[None, None, :, None])
    hidden_lines = hidden.reshape(lines_dev, channels, NZ)
    query_slots = slot_rows(dec_dest[:, 0], slab_count, capacity)
    query_source, query_filled = find_source(query_slots, slot_total)
    requests = jnp.where(query_filled, dec_line[query_source], -1)
    positions = jnp.where(query_filled[:, None, None], dec_pos[query_source], 0.0)
    got_positions, got_requests = (
        lax.all_to_all(positions, "slab", split_axis=0, concat_axis=0, tiled=True),
        lax.all_to_all(requests, "slab", split_axis=0, concat_axis=0, tiled=True),
    )
    fetched = hidden_lines[jnp.maximum(got_requests, 0)]
    answers = decode_blocks(fetched, got_positions, dec_weight, out_weight)
    returned = lax.all_to_all(answers, "slab", split_axis=0, concat_axis=0, tiled=True)
    pressure = returned[query_slots]
    return pressure


def solution(mesh):
    placed = (
        P(("geo", "slab"), None, None),
        P(("geo", "slab"), None, None),
        P(("geo", "slab"), None),
        P(("geo", "slab")),
        P(("geo", "slab"), None, None),
        P(("geo", "slab"), None),
        P(("geo", "slab")),
        P(None, "slab", None, None),
        P(),
        P(),
        P(),
        P(),
    )
    return jax.shard_map(
        local, mesh=mesh, in_specs=placed, out_specs=P(("geo", "slab"), None), check_vma=False
    )
```

profile of v0, /device:TPU:1, one launch (start us, length us, event | category | flops | bytes accessed | tf_op | source)
XLA Modules:
  0.0 553.7 jit_solution(14189621525776176040)
XLA Ops:
  2.7 3.4 gather_fusion
  6.9 13.0 %all-to-all-start = ((s32[64,6,1]{1,2,0:T(1,128)}), s32[64,6,1]{1,2,0:T(1,128)S(1)}, u32[]{:S(2)}, u32[]{:S(2)}) async-start(s32[64,6,1]{1,2,0:T(1,128)} %bitcast.9), calls=%async_computation | async-start | bytes 65536 | tf_op jit(solution)/shard_map/all_to_all | solution.py:98
  20.9 12.0 %fusion.45 = f32[128,32,128]{2,1,0:T(8,128)} fusion(f32[128,32,128]{2,1,0:T(8,128)S(1)} %copy-done, f32[128,128]{1,0:T(8,128)S(1)} %get-tuple-element.27, f32[128,128]{1,0:T(8,128)S(1)} %get-tuple-element.26), kind=kOutput, calls=%fused_computation.62 | convolution fusion | flops 815792128 | bytes 4325376 | tf_op jit(solution)/shard_map/bcp,bpz->bcz/dot_general | solution.py:68
  32.9 5.2 gather_fusion.1
  38.1 5.2 broadcast_select_fusion
  43.3 10.8 %all-to-all-start.1 = ((f32[384,32,128]{2,1,0:T(8,128)}), f32[384,32,128]{2,1,0:T(8,128)}, u32[]{:S(2)}, u32[]{:S(2)}) async-start(f32[384,32,128]{2,1,0:T(8,128)} %broadcast_select_fusion), calls=%async_computation.1 | async-start | bytes 12582912 | tf_op jit(solution)/shard_map/all_to_all | solution.py:97
  55.6 139.2 %all-to-all-done.1 = f32[384,32,128]{2,1,0:T(8,128)} async-done(((f32[384,32,128]{2,1,0:T(8,128)}), f32[384,32,128]{2,1,0:T(8,128)}, u32[]{:S(2)}, u32[]{:S(2)}) %all-to-all-start.1) | async-done | bytes 6291488 | tf_op jit(solution)/shard_map/all_to_all | solution.py:97
  194.8 2.6 broadcast_in_dim.38
  197.3 54.2 %scatter_fusion = f32[257,32,128]{2,1,0:T(8,128)} fusion(f32[257,32,128]{2,1,0:T(8,128)} %broadcast_in_dim.38, s32[384]{0:T(512)S(1)} %fusion.150, f32[384,32,128]{2,1,0:T(8,128)} %all-to-all-done.1), kind=kCustom, calls=%fused_computation.6 | custom fusion | flops 1572864 | bytes 18875904 | tf_op jit(solution)/shard_map/scatter-add | solution.py:101
  251.6 2.6 slice.64
  254.2 5.2 fusion.111
  259.4 5.2 fusion.109
  264.6 3.8 copy.197
  268.4 5.0 copy.198
  276.1 1.9 fusion.54
  278.0 1.9 fusion.52
  281.6 3.0 copy.202
  284.6 4.4 copy.203
  289.0 6.2 %all-to-all-start.2 = ((f32[2,64,2112]{2,0,1:T(2,128)}), f32[2,64,2112]{2,0,1:T(2,128)S(1)}, u32[]{:S(2)}, u32[]{:S(2)}) async-start(f32[2,64,2112]{2,0,1:T(2,128)} %copy.203), calls=%async_computation.2 | async-start | bytes 2228224 | tf_op jit(solution)/shard_map/all_to_all | solution.py:115
  295.2 16.3 %copy.206 = bf16[64,1,33,2048]{0,3,2,1:T(8,128)(2,1)} copy(bf16[64,1,33,2048]{3,0,2,1:T(8,128)(2,1)} %param.19) | data formatting | bytes 17301504 | tf_op args[7]
  312.2 2.7 gather_fusion.2
  315.7 2.3 gather_fusion.4
  319.4 5.6 %all-to-all-done.2 = f32[2,64,2112]{2,0,1:T(2,128)S(1)} async-done(((f32[2,64,2112]{2,0,1:T(2,128)}), f32[2,64,2112]{2,0,1:T(2,128)S(1)}, u32[]{:S(2)}, u32[]{:S(2)}) %all-to-all-start.2) | async-done | bytes 1081376 | tf_op jit(solution)/shard_map/all_to_all | solution.py:115
  325.0 6.2 %all-to-all-start.4 = ((s32[64,6,1]{1,2,0:T(1,128)}), s32[64,6,1]{1,2,0:T(1,128)S(1)}, u32[]{:S(2)}, u32[]{:S(2)}) async-start(s32[64,6,1]{1,2,0:T(1,128)} %bitcast.61), calls=%async_computation.4 | async-start | bytes 65536 | tf_op jit(solution)/shard_map/all_to_all | solution.py:165
  331.2 7.1 %reshape.296 = f32[128,1,2,32,33]{4,3,2,0,1:T(8,128)} reshape(f32[64,2,1,2112]{3,1,0,2:T(2,128)S(1)} %bitcast.207) | data formatting | bytes 2162688 | tf_op jit(solution)/shard_map/reshape | solution.py:117
  338.2 4.1 fusion.240
  342.3 2.7 copy.257
  345.0 1.7 fusion.71
  348.9 2.0 fusion.59
  352.0 10.5 %all-to-all-start.5 = ((f32[384,3,128]{2,1,0:T(4,128)}), f32[384,3,128]{2,1,0:T(4,128)}, u32[]{:S(2)}, u32[]{:S(2)}) async-start(f32[384,3,128]{2,1,0:T(4,128)} %copy.217), calls=%async_computation.5 | async-start | bytes 1572864 | tf_op jit(solution)/shard_map/all_to_all | solution.py:164
  362.5 15.0 %fusion.10 = (f32[64,33,32]{0,2,1:T(8,128)S(1)}, f32[64,33,32]{0,2,1:T(8,128)S(1)}, f32[64,33,32]{0,2,1:T(8,128)S(1)}, f32[64,33,32]{0,2,1:T(8,128)S(1)}) fusion(f32[64,33,32]{0,2,1:T(8,128)S(1)} %copy.262, bf16[64,1,33,2,32,32]{0,5,4,3,2,1:T(8,128)(2,1)} %bitcast.200, f32[64,33,32]{0,2,1:T(8,128)S(1)} %copy.263), kind=kLoop, calls=%fused_computation.21 | loop fusion | flops 21356544 | bytes 10272768
  379.2 1.7 fusion.62
  385.3 3.7 copy.207
  389.1 10.3 %all-to-all-start.3 = ((f32[128,1,2112]{2,1,0:T(1,128)}), f32[128,1,2112]{2,1,0:T(1,128)S(1)}, u32[]{:S(2)}, u32[]{:S(2)}) async-start(f32[128,1,2112]{2,1,0:T(1,128)} %copy.207), calls=%async_computation.3 | async-start | bytes 2228224 | tf_op jit(solution)/shard_map/all_to_all | solution.py:142
  399.6 2.4 fusion.242
  402.1 7.8 %fusion.120 = f32[2,128,128,32]{2,3,1,0:T(8,128)} fusion(f32[2,128,32,128]{3,2,1,0:T(8,128)} %bitcast.203, f32[32,32]{1,0:T(8,128)S(1)} %copy-done.6), kind=kOutput, calls=%fused_computation.170 | convolution fusion | flops 402653184 | bytes 8392704 | tf_op jit(solution)/shard_map/xycn,cd->xydn/dot_general | solution.py:68
  409.9 19.4 %all-to-all-done.3 = f32[128,1,2112]{2,1,0:T(1,128)S(1)} async-done(((f32[128,1,2112]{2,1,0:T(1,128)}), f32[128,1,2112]{2,1,0:T(1,128)S(1)}, u32[]{:S(2)}, u32[]{:S(2)}) %all-to-all-start.3) | async-done | bytes 1081376 | tf_op jit(solution)/shard_map/all_to_all | solution.py:142
  429.3 3.6 copy.208
  432.9 1.7 fusion.241
  440.2 6.9 %fusion.107 = f32[2,128,32,128]{3,1,2,0:T(8,128)S(1)} fusion(f32[2,128,32,33]{1,3,2,0:T(8,128)S(1)} %fusion.51, f32[33]{0:T(128)S(1)} %fusion.151), kind=kOutput, calls=%fused_computation.157 | convolution fusion | flops 415299456 | bytes 5275780 | tf_op jit(solution)/shard_map/xyck,nk->xycn/dot_general | solution.py:68
  447.1 11.6 %fusion.36 = f32[2,128,32,128]{3,1,2,0:T(8,128)S(1)} fusion(f32[2,128,128,32]{2,3,1,0:T(8,128)S(1)} %copy-done.5, f32[2,128,32,128]{3,1,2,0:T(8,128)S(1)} %fusion.107, f32[2,128,32,33]{1,3,2,0:T(8,128)S(1)} %fusion.49, f32[32]{0:T(128)S(1)} %copy-done.8, f32[33]{0:T(128)S(1)} %fusion.151), kind=kOutput, calls=%fused_computation.50 | convolution fusion | flops 426833792 | bytes 13664516 | tf_op jit(solution)/shard_map/xyck,nk->xycn/dot_general | solution.py:68
  458.7 4.5 copy.213
  463.2 5.8 %gather_fusion.3 = f32[384,32,128]{2,1,0:T(8,128)} fusion(f32[256,32,128]{2,1,0:T(8,128)} %bitcast.204, s32[1024]{0:T(1024)S(1)} %pad_clamp_fusion.1), kind=kCustom, calls=%fused_computation.3 | custom fusion | bytes 12584448 | tf_op jit(solution)/shard_map/gather | solution.py:167
  469.0 53.0 %fusion.3 = f32[384,32,128]{2,1,0:T(8,128)S(1)} fusion(f32[384,32,128]{2,1,0:T(8,128)} %gather_fusion.3, f32[384,128]{1,0:T(8,128)S(1)} %bitcast.211, f32[384,128]{1,0:T(8,128)S(1)} %exponential_bitcast_fusion), kind=kOutput, calls=%fused_computation.11 | convolution fusion | flops 2447376384 | bytes 12976128 | tf_op jit(solution)/shard_map/bcz,bpz->bcp/dot_general | solution.py:43
  522.1 6.1 %fusion.118 = f32[384,128,32]{1,2,0:T(8,128)S(1)} fusion(f32[384,32,128]{2,1,0:T(8,128)S(1)} %fusion.3, f32[32,32]{1,0:T(8,128)S(1)} %copy-done.7), kind=kOutput, calls=%fused_computation.168 | convolution fusion | flops 603979776 | bytes 12587008 | tf_op jit(solution)/shard_map/bcp,cd->bdp/dot_general | solution.py:45
  528.2 5.1 fusion.28
  534.0 6.2 %all-to-all-start.6 = ((f32[64,6,128]{2,1,0:T(8,128)}), f32[64,6,128]{2,1,0:T(8,128)S(1)}, u32[]{:S(2)}, u32[]{:S(2)}) async-start(f32[64,6,128]{2,1,0:T(8,128)} %all_to_all.57), calls=%async_computation.6 | async-start | bytes 524288 | tf_op jit(solution)/shard_map/all_to_all | solution.py:169
  540.2 11.9 %all-to-all-done.6 = f32[64,6,128]{2,1,0:T(8,128)S(1)} async-done(((f32[64,6,128]{2,1,0:T(8,128)}), f32[64,6,128]{2,1,0:T(8,128)S(1)}, u32[]{:S(2)}, u32[]{:S(2)}) %all-to-all-start.6) | async-done | bytes 196640 | tf_op jit(solution)/shard_map/all_to_all | solution.py:169
  (83 shorter events, 30.1 us)
Async XLA Ops:
  0.0 20.9 %copy-start = (f32[128,32,128]{2,1,0:T(8,128)S(1)}, f32[128,32,128]{2,1,0:T(8,128)}, u32[]{:S(2)}) copy-start(f32[128,32,128]{2,1,0:T(8,128)} %param.12) | copy-start | bytes 6291460
  6.9 36.4 %all-to-all-start = ((s32[64,6,1]{1,2,0:T(1,128)}), s32[64,6,1]{1,2,0:T(1,128)S(1)}, u32[]{:S(2)}, u32[]{:S(2)}) async-start(s32[64,6,1]{1,2,0:T(1,128)} %bitcast.9), calls=%async_computation | async-start | bytes 65536 | tf_op jit(solution)/shard_map/all_to_all | solution.py:98
  43.3 151.5 %all-to-all-start.1 = ((f32[384,32,128]{2,1,0:T(8,128)}), f32[384,32,128]{2,1,0:T(8,128)}, u32[]{:S(2)}, u32[]{:S(2)}) async-start(f32[384,32,128]{2,1,0:T(8,128)} %broadcast_select_fusion), calls=%async_computation.1 | async-start | bytes 12582912 | tf_op jit(solution)/shard_map/all_to_all | solution.py:97
  254.2 5.2 copy-start.4
  289.0 36.0 %all-to-all-start.2 = ((f32[2,64,2112]{2,0,1:T(2,128)}), f32[2,64,2112]{2,0,1:T(2,128)S(1)}, u32[]{:S(2)}, u32[]{:S(2)}) async-start(f32[2,64,2112]{2,0,1:T(2,128)} %copy.203), calls=%async_computation.2 | async-start | bytes 2228224 | tf_op jit(solution)/shard_map/all_to_all | solution.py:115
  295.2 16.4 %copy-start.9 = (s32[128,1]{0,1:T(1,128)S(1)}, s32[128,1]{0,1:T(1,128)}, u32[]{:S(2)}) copy-start(s32[128,1]{0,1:T(1,128)} %param.17) | copy-start | bytes 1540
  295.2 17.0 %copy-start.2 = (s32[128]{0:T(128)S(1)}, s32[128]{0:T(128)}, u32[]{:S(2)}) copy-start(s32[128]{0:T(128)} %param.18) | copy-start | bytes 1540
  311.5 4.1 copy-start.3
  325.0 27.0 %all-to-all-start.4 = ((s32[64,6,1]{1,2,0:T(1,128)}), s32[64,6,1]{1,2,0:T(1,128)S(1)}, u32[]{:S(2)}, u32[]{:S(2)}) async-start(s32[64,6,1]{1,2,0:T(1,128)} %bitcast.61), calls=%async_computation.4 | async-start | bytes 65536 | tf_op jit(solution)/shard_map/all_to_all | solution.py:165
  352.0 37.1 %all-to-all-start.5 = ((f32[384,3,128]{2,1,0:T(4,128)}), f32[384,3,128]{2,1,0:T(4,128)}, u32[]{:S(2)}, u32[]{:S(2)}) async-start(f32[384,3,128]{2,1,0:T(4,128)} %copy.217), calls=%async_computation.5 | async-start | bytes 1572864 | tf_op jit(solution)/shard_map/all_to_all | solution.py:164
  384.2 17.8 %copy-start.6 = (f32[32,32]{1,0:T(8,128)S(1)}, f32[32,32]{1,0:T(8,128)}, u32[]{:S(2)}) copy-start(f32[32,32]{1,0:T(8,128)} %param.20) | copy-start | bytes 12292
  389.1 40.3 %all-to-all-start.3 = ((f32[128,1,2112]{2,1,0:T(1,128)}), f32[128,1,2112]{2,1,0:T(1,128)S(1)}, u32[]{:S(2)}, u32[]{:S(2)}) async-start(f32[128,1,2112]{2,1,0:T(1,128)} %copy.207), calls=%async_computation.3 | async-start | bytes 2228224 | tf_op jit(solution)/shard_map/all_to_all | solution.py:142
  440.2 7.0 %copy-start.5 = (f32[2,128,128,32]{2,3,1,0:T(8,128)S(1)}, f32[2,128,128,32]{2,3,1,0:T(8,128)}, u32[]{:S(2)}) copy-start(f32[2,128,128,32]{2,3,1,0:T(8,128)} %fusion.120) | copy-start | bytes 12582916
  440.2 7.0 %copy-start.8 = (f32[32]{0:T(128)S(1)}, f32[32]{0:T(128)}, u32[]{:S(2)}) copy-start(f32[32]{0:T(128)} %param.21) | copy-start | bytes 388
  469.0 53.0 %copy-start.7 = (f32[32,32]{1,0:T(8,128)S(1)}, f32[32,32]{1,0:T(8,128)}, u32[]{:S(2)}) copy-start(f32[32,32]{1,0:T(8,128)} %param.22) | copy-start | bytes 12292
  522.1 6.1 %copy-start.10 = (f32[32]{0:T(128)S(1)}, f32[32]{0:T(128)}, u32[]{:S(2)}) copy-start(f32[32]{0:T(128)} %param.23) | copy-start | bytes 388
  528.2 25.3 %copy-start.1 = (f32[128,32,128]{2,1,0:T(8,128)S(1)}, f32[128,32,128]{2,1,0:T(8,128)}, u32[]{:S(2)}) copy-start(f32[128,32,128]{2,1,0:T(8,128)} %param.12) | copy-start | bytes 6291460
  534.0 18.2 %all-to-all-start.6 = ((f32[64,6,128]{2,1,0:T(8,128)}), f32[64,6,128]{2,1,0:T(8,128)S(1)}, u32[]{:S(2)}, u32[]{:S(2)}) async-start(f32[64,6,128]{2,1,0:T(8,128)} %all_to_all.57), calls=%async_computation.6 | async-start | bytes 524288 | tf_op jit(solution)/shard_map/all_to_all | solution.py:169
where the time goes:
time: 560 us; the launch traced here: 554 us
  waiting for transfers between devices  176 us (31%)
  matrix products  137 us (24%)
  local copies, waits for them, and re-layouts  93.1 us (17%)
  other arithmetic  83.4 us (15%)
  starting transfers between devices  63.2 us (11%)
    all_to_all x1, waiting for transfers between devices, local(): lax.all_to_all(packed, 'slab', split_axis=0, concat_axis=0, tiled=True)  139 us
    dot_general x22, matrix products, einsum_exact(): return jnp.einsum(form, left, right, precision=lax.Precision.HIGHEST)  72.7 us
    scatter-add x1, other arithmetic, local(): jax.ops.segment_sum(got_terms, target, num_segments=lines_dev + 1)  54.2 us
    dot_general x1, matrix products, decode_blocks(): jnp.einsum('bcz,bpz->bcp', line_data, kernel, precision=lax.Precision.HIG...  53 us
    unnamed x27, local copies, waits for them, and re-layouts  20.6 us
    all_to_all x1, waiting for transfers between devices, local(): lax.all_to_all(inverse, 'slab', split_axis=0, concat_axis=1, tiled=True)  19.4 us
    unnamed x1, other arithmetic  15 us
    all_to_all x1, starting transfers between devices, local(): lax.all_to_all(line_ids, 'slab', split_axis=0, concat_axis=0, tiled=True)  13 us
  transfers between devices with their start and end apart: 7, of which 4 were waited for; matrix products, arithmetic and copies ran while one was open for 19% of the time, Pallas kernels for 0%

commit v1 on v0

v1 whole, which is shorter than its diff:
```python
import functools
import math

import jax
import jax.numpy as jnp
import numpy as np
from jax import lax
from jax.experimental import pallas as pl
from jax.experimental.pallas import tpu as pltpu
from jax.sharding import PartitionSpec as P

C = 32
NX = 128
NY = 128
NZ = 128
MX = 64
MY = 64
MZ = 33
PB = 128
BLK = 128
SLABS = 64
PLANES = NX // SLABS
CAP = 6
SLOTS = SLABS * CAP
LINES = PLANES * NY
MROWS = 40
QROWS = 24
VMEM_LIMIT = 60 * 1024 * 1024

radius_scale = 0.7
spread_cells = 1.5
BF = jnp.bfloat16
F32 = jnp.float32


def split_np(table):
    table = np.asarray(table, np.float32)
    high = table.astype(jnp.bfloat16)
    low = (table - high.astype(np.float32)).astype(jnp.bfloat16)
    return high, low


def split(values):
    high = values.astype(BF)
    low = (values - high.astype(F32)).astype(BF)
    return high, low


def split_table(values):
    high = lax.reduce_precision(values, 8, 7)
    return high.astype(BF), (values - high).astype(BF)


def mm(left, right):
    return jnp.dot(left, right, preferred_element_type=F32)


def mm3(left, right):
    return mm(left[0], right[0]) + (mm(left[1], right[0]) + mm(left[0], right[1]))


def nt(left, right):
    return lax.dot_general(left, right, (((1,), (1,)), ((), ())), preferred_element_type=F32)


def kept(length, count):
    counter = np.arange(count)
    return np.where(counter < count // 2, counter, counter + length - count)


def tables():
    cells = np.arange(NY)
    ky = kept(NY, MY)
    angle = 2.0 * math.pi * ((ky[:, None] * cells[None, :]) % NY) / NY
    cos_y, sin_y = np.cos(angle), np.sin(angle)
    forward_y = np.concatenate([cos_y, -sin_y], axis=0)
    inverse_y = np.concatenate([cos_y.T, sin_y.T], axis=0) / NY
    z_angle = 2.0 * math.pi * ((np.arange(NZ)[:, None] * np.arange(MZ)[None, :]) % NZ) / NZ
    cos_z, sin_z = np.cos(z_angle), np.sin(z_angle)
    forward_z = np.zeros((2 * NZ, 128))
    forward_z[:NZ, :MZ] = cos_z
    forward_z[:NZ, 64 : 64 + MZ] = -sin_z
    forward_z[NZ:, :MZ] = sin_z
    forward_z[NZ:, 64 : 64 + MZ] = cos_z
    weight = np.where(np.arange(MZ) == 0, 1.0, 2.0) / NZ
    inverse_z = np.zeros((2, 2, 64, 2, NZ))
    for twin in range(2):
        inverse_z[0, twin, :MZ, twin, :] = (cos_z * weight[None, :]).T
        inverse_z[1, twin, :MZ, twin, :] = -(sin_z * weight[None, :]).T
    inverse_z = inverse_z.reshape(256, 256)
    kx = kept(NX, MX)
    owner = np.arange(SLABS)
    forward_x, inverse_x = [], []
    for part in (np.cos, np.sin):
        for plane in range(PLANES):
            turns = (kx[:, None] * (PLANES * owner + plane)[None, :]) % NX
            table = part(2.0 * math.pi * turns / NX)
            forward_x.append(table)
            inverse_x.append(table.T / NX)
    forward_x = np.concatenate(forward_x, axis=0)
    inverse_x = np.concatenate(inverse_x, axis=0)
    spread = np.zeros((2, PLANES, C, 2, C, C))
    for channel in range(C):
        for part in range(2):
            spread[part, :, channel, part, channel, :] = 1.0
    spread = spread.reshape(128, 2 * C * C)
    gather = np.zeros((2, 4, C, 2, PLANES, C))
    for channel in range(C):
        for part in range(2):
            gather[part, :, channel, part, :, channel] = 1.0
    gather = gather.reshape(256, 128)
    return (
        split_np(forward_y),
        split_np(inverse_y),
        split_np(forward_z),
        split_np(inverse_z),
        split_np(forward_x),
        split_np(inverse_x),
        np.asarray(spread, jnp.bfloat16),
        np.asarray(gather, jnp.bfloat16),
    )


def params(**extra):
    return pltpu.CompilerParams(vmem_limit_bytes=VMEM_LIMIT, **extra)


def whole(shape):
    return pl.BlockSpec(shape, lambda *_: (0,) * len(shape))


SMEM = pl.BlockSpec(memory_space=pltpu.SMEM)


def routes_kernel(ed_r, ed_c, el_c, dd_r, dd_c, dl_c, out):
    def one(dest_r, dest_c, line_c):
        same = dest_c == dest_r
        rows = lax.broadcasted_iota(jnp.int32, (BLK, BLK), 0)
        cols = lax.broadcasted_iota(jnp.int32, (BLK, BLK), 1)
        before_r = jnp.sum(jnp.where(same & (rows < cols), 1.0, 0.0), axis=0, keepdims=True)
        before_c = jnp.sum(jnp.where(same & (cols < rows), 1.0, 0.0), axis=1, keepdims=True)
        slot_r = dest_r * CAP + before_r.astype(jnp.int32)
        slot_c = dest_c * CAP + before_c.astype(jnp.int32)
        match = slot_c == lax.broadcasted_iota(jnp.int32, (BLK, SLOTS), 1)
        number = lax.broadcasted_iota(jnp.int32, (BLK, SLOTS), 0).astype(F32)
        filled = jnp.sum(jnp.where(match, 1.0, 0.0), axis=0, keepdims=True)
        source = jnp.sum(jnp.where(match, number, 0.0), axis=0, keepdims=True)
        line = jnp.sum(jnp.where(match, line_c.astype(F32), 0.0), axis=0, keepdims=True)
        return slot_r, filled, source.astype(jnp.int32), line.astype(jnp.int32)

    out[...] = jnp.zeros((8, SLOTS), jnp.int32)
    _, filled, source, line = one(ed_r[...], ed_c[...], el_c[...])
    out[0:1, :] = jnp.where(filled > 0.5, source, BLK)
    out[1:2, :] = line
    slot, _, source, line = one(dd_r[...], dd_c[...], dl_c[...])
    out[2:3, :] = source
    out[3:4, :] = line
    out[4:5, 0:BLK] = slot


def encode_kernel(route, feat, pos, out, terms):
    step = pl.program_id(0)

    @pl.when(step == 0)
    def _():
        terms[BLK] = jnp.zeros((C, NZ), F32)

    @pl.when(step < 8)
    def _():
        grid_cells = lax.broadcasted_iota(jnp.int32, (NZ, PB), 0).astype(F32)
        for b in range(16):
            a, o, t = pos[b, 0:1, :], pos[b, 1:2, :], pos[b, 2:3, :]
            radial = jnp.exp((a * a + o * o) * (-1.0 / (2.0 * radius_scale**2)))
            offset = grid_cells - (t + 1.0) * (0.5 * (NZ - 1))
            rows = jnp.exp(offset * offset * (-1.0 / (2.0 * spread_cells**2)))
            fh, fl = split(feat[b] * radial)
            kh, kl = split(rows)
            both = nt(jnp.concatenate([fh, fl], axis=0), kh)
            terms[step * 16 + b] = both[:C] + (both[C:] + nt(fh, kl))

    @pl.when(step >= 8)
    def _():
        base = (step - 8) * 48

        def put(i, carry):
            out[i] = terms[route[0, base + i]]
            return carry

        lax.fori_loop(0, 48, put, 0, unroll=8)


def queries_kernel(route, pos, out):
    lane = lax.broadcasted_iota(jnp.int32, (1, 128), 1)

    def peer(d, carry):
        tags = jnp.zeros((1, 128), F32)
        for r in range(CAP):
            s = d * CAP + r
            out[d, 3 * r : 3 * r + 3, :] = pos[route[2, s]]
            tags = jnp.where(lane == r, route[3, s].astype(F32), tags)
            tags = jnp.where(lane == CAP + r, route[1, s].astype(F32), tags)
        out[d, 18:19, :] = tags
        out[d, 19:24, :] = jnp.zeros((5, 128), F32)
        return carry

    lax.fori_loop(0, SLABS, peer, 0)


def forward_kernel(tags, got, dyh, dyl, zh, zl, latent, message, scratch):
    step = pl.program_id(0)

    @pl.when(step == 0)
    def _():
        latent[...] = jnp.zeros_like(latent)

    for q in range(8):
        for r in range(CAP):
            line = tags[step * 8 + q, CAP + r]
            start = pl.multiple_of(line * C, C)
            latent[pl.ds(start, C), :] += got[q * CAP + r]

    @pl.when(step == 7)
    def _():
        def pair(i, carry):
            plane = i // (C // 2)
            channel = (i % (C // 2)) * 2
            start = plane * NY * C + channel
            first = latent[pl.ds(start, NY, stride=C), :]
            second = latent[pl.ds(start + 1, NY, stride=C), :]
            data = split(jnp.concatenate([first, second], axis=1))
            y = mm3((dyh[...], dyl[...]), data)
            x = jnp.concatenate(
                [
                    jnp.concatenate([y[:MY, :NZ], y[MY:, :NZ]], axis=1),
                    jnp.concatenate([y[:MY, NZ:], y[MY:, NZ:]], axis=1),
                ],
                axis=0,
            )
            s = mm3(split(x), (zh[...], zl[...]))
            at = pl.multiple_of((plane * C + channel) * MY, MY)
            scratch[pl.ds(at, 2 * MY), :] = s
            return carry

        lax.fori_loop(0, PLANES * C // 2, pair, 0, unroll=2)

        def flip(j, carry):
            turned = jnp.transpose(scratch[pl.ds(j, PLANES * C, stride=MY), :])
            message[j, :, 0:64] = turned[:MROWS]
            message[j, :, 64:128] = turned[64 : 64 + MROWS]
            return carry

        lax.fori_loop(0, MY, flip, 0, unroll=2)


def skip_kernel(kh, kl, bias, latent, out):
    data = split(latent[...])
    out[...] = mm3((kh[...], kl[...]), data) + bias[...]


def mix_kernel(spec, weight, xh, xl, spread, gather, ih, il, out):
    step = pl.program_id(0)
    lane = lax.broadcasted_iota(jnp.int32, (64, 128), 1)
    first_plane = (lane & 32) == 0
    real_part = lane < 64
    for sub in range(3):
        kz = step * 3 + sub
        data = split(spec[pl.ds(kz, SLABS, stride=MROWS), :])
        t = mm3((xh[...], xl[...]), data)
        u = jnp.where(first_plane, t[0:64], t[64:128])
        w = pltpu.roll(jnp.where(first_plane, t[128:192], t[192:256]), 64, 1)
        s = u + jnp.where(real_part, w, -w)
        sh, sl = split(s)
        wide = mm(sh, spread[...]) + mm(sl, spread[...])
        acc_re = jnp.zeros((64, 128), F32)
        acc_im = jnp.zeros((64, 128), F32)
        for piece in range(8):
            re = slice(piece * 128, piece * 128 + 128)
            im = slice(C * C + piece * 128, C * C + piece * 128 + 128)
            w_re = weight[sub, :, re].astype(F32)
            w_im = weight[sub, :, im].astype(F32)
            acc_re += wide[:, re] * w_re - wide[:, im] * w_im
            acc_im += wide[:, re] * w_im + wide[:, im] * w_re
        ah, al = split(jnp.concatenate([acc_re, acc_im], axis=1))
        o = mm(ah, gather[...]) + mm(al, gather[...])
        t = mm3((ih[...], il[...]), split(o))
        u = jnp.where(first_plane, t[0:64], t[64:128])
        w = pltpu.roll(jnp.where(first_plane, t[128:192], t[192:256]), 64, 1)
        out[pl.ds(kz, SLABS, stride=MROWS), :] = u + jnp.where(real_part, -w, w)


def decode_kernel(tags, inverse, base, pos, yh, yl, zh, zl, dh, dl, oh, ol, out, modes, hidden):
    lane = lax.broadcasted_iota(jnp.int32, (NY, 128), 1)
    real_part = lane < 64

    def clear(n, carry):
        modes[pl.ds(pl.multiple_of(n * 64 + 32, 32), 32), :] = jnp.zeros((32, 128), F32)
        return carry

    lax.fori_loop(0, NY, clear, 0, unroll=8)

    def planes(k, carry):
        data = split(inverse[pl.ds(k, MY, stride=MROWS), :])
        t = mm3((yh[...], yl[...]), data)
        w = pltpu.roll(t[NY:], 64, 1)
        modes[pl.ds(k, NY, stride=64), :] = t[:NY] + jnp.where(real_part, -w, w)
        return carry

    lax.fori_loop(0, MZ, planes, 0, unroll=3)

    def columns(i, carry):
        turned = jnp.transpose(modes[pl.ds(pl.multiple_of(i * 128, 128), 128), :])
        x = split(jnp.concatenate([turned[:64], turned[64:]], axis=1))
        s = mm3(x, (zh[...], zl[...]))
        for plane in range(PLANES):
            for twin in range(2):
                at = pl.multiple_of((plane * NY + 2 * i + twin) * C, C)
                rows = slice(plane * C, plane * C + C)
                value = s[rows, twin * NZ : twin * NZ + NZ] + base[pl.ds(at, C), :]
                hidden[pl.ds(at, C), :] = jax.nn.gelu(value)
        return carry

    lax.fori_loop(0, NY // 2, columns, 0, unroll=2)

    grid_cells = lax.broadcasted_iota(jnp.int32, (NZ, PB), 0).astype(F32)

    def answer(g, carry):
        near = []
        for i in range(8):
            s = g * 8 + i
            d = s // CAP
            r = s - d * CAP
            line = tags[d, r]
            row = d * QROWS + 3 * r
            a = pos[pl.ds(row, 1), :]
            o = pos[pl.ds(row + 1, 1), :]
            t = pos[pl.ds(row + 2, 1), :]
            radial = jnp.exp((a * a + o * o) * (-1.0 / (2.0 * radius_scale**2)))
            offset = grid_cells - (t + 1.0) * (0.5 * (NZ - 1))
            rows = jnp.exp(offset * offset * (-1.0 / (2.0 * spread_cells**2)))
            kh, kl = split(rows)
            hh, hl = split(hidden[pl.ds(pl.multiple_of(line * C, C), C), :])
            both = mm(jnp.concatenate([hh, hl], axis=0), kh)
            near.append((both[:C] + (both[C:] + mm(hh, kl))) * radial)
        nearby = split(jnp.concatenate(near, axis=0))
        act = split(jax.nn.gelu(mm3((dh[...], dl[...]), nearby)))
        out[pl.ds(pl.multiple_of(g * 8, 8), 8), :] = mm3((oh[...], ol[...]), act)
        return carry

    lax.fori_loop(0, SLOTS // 8, answer, 0)


def local(
    enc_feat,
    enc_pos,
    enc_dest,
    enc_line,
    dec_pos,
    dec_dest,
    dec_line,
    mode_weight,
    skip_weight,
    skip_bias,
    dec_weight,
    out_weight,
):
    forward_y, inverse_y, forward_z, inverse_z, forward_x, inverse_x, spread, gather = tables()
    exchange = functools.partial(
        lax.all_to_all, axis_name="slab", split_axis=0, concat_axis=0, tiled=True
    )
    route = pl.pallas_call(
        routes_kernel, out_shape=jax.ShapeDtypeStruct((8, SLOTS), jnp.int32), name="routes"
    )(
        enc_dest.reshape(1, BLK),
        enc_dest,
        enc_line.reshape(BLK, 1),
        dec_dest.reshape(1, BLK),
        dec_dest,
        dec_line.reshape(BLK, 1),
    )
    queries = pl.pallas_call(
        queries_kernel,
        out_shape=jax.ShapeDtypeStruct((SLABS, QROWS, 128), F32),
        in_specs=[SMEM, whole((BLK, 3, PB))],
        out_specs=whole((SLABS, QROWS, 128)),
        name="queries",
    )(route, dec_pos)
    packed = pl.pallas_call(
        encode_kernel,
        out_shape=jax.ShapeDtypeStruct((SLOTS, C, NZ), F32),
        grid=(16,),
        in_specs=[
            SMEM,
            pl.BlockSpec((16, C, PB), lambda i: (jnp.minimum(i, 7), 0, 0)),
            pl.BlockSpec((16, 3, PB), lambda i: (jnp.minimum(i, 7), 0, 0)),
        ],
        out_specs=pl.BlockSpec((48, C, NZ), lambda i: (jnp.maximum(i - 8, 0), 0, 0)),
        scratch_shapes=[pltpu.VMEM((BLK + 1, C, NZ), F32)],
        compiler_params=params(),
        name="encode",
    )(route, enc_feat, enc_pos)
    got_queries = exchange(queries)
    got_terms = exchange(packed)
    tags = got_queries[:, 18, 0 : 2 * CAP].astype(jnp.int32)
    latent, message = pl.pallas_call(
        forward_kernel,
        out_shape=(
            jax.ShapeDtypeStruct((LINES * C, NZ), F32),
            jax.ShapeDtypeStruct((MY, MROWS, 128), F32),
        ),
        grid=(8,),
        in_specs=[
            SMEM,
            pl.BlockSpec((48, C, NZ), lambda i: (i, 0, 0)),
            whole((2 * MY, NY)),
            whole((2 * MY, NY)),
            whole((2 * NZ, 128)),
            whole((2 * NZ, 128)),
        ],
        out_specs=(whole((LINES * C, NZ)), whole((MY, MROWS, 128))),
        scratch_shapes=[pltpu.VMEM((PLANES * C * MY, 128), F32)],
        compiler_params=params(),
        name="forward",
    )(tags, got_terms, *forward_y, *forward_z)
    spectrum = exchange(message)
    skip_wide = jnp.kron(jnp.eye(8, dtype=F32), skip_weight.T)
    base = pl.pallas_call(
        skip_kernel,
        out_shape=jax.ShapeDtypeStruct((LINES * C, NZ), F32),
        grid=(32,),
        in_specs=[
            whole((256, 256)),
            whole((256, 256)),
            whole((256, 1)),
            pl.BlockSpec((256, NZ), lambda i: (i, 0)),
        ],
        out_specs=pl.BlockSpec((256, NZ), lambda i: (i, 0)),
        compiler_params=params(),
        name="skip",
    )(*split_table(skip_wide), jnp.tile(skip_bias, 8)[:, None], latent)
    weight = jnp.transpose(mode_weight.reshape(MX, MZ, 2 * C * C), (1, 0, 2))
    mixed = pl.pallas_call(
        mix_kernel,
        out_shape=jax.ShapeDtypeStruct((SLABS * MROWS, 128), F32),
        grid=(11,),
        in_specs=[
            whole((SLABS * MROWS, 128)),
            pl.BlockSpec((3, MX, 2 * C * C), lambda i: (i, 0, 0)),
            whole((256, 64)),
            whole((256, 64)),
            whole((128, 2 * C * C)),
            whole((256, 128)),
            whole((256, 64)),
            whole((256, 64)),
        ],
        out_specs=whole((SLABS * MROWS, 128)),
        compiler_params=params(),
        name="mix",
    )(spectrum.reshape(SLABS * MROWS, 128), weight, *forward_x, spread, gather, *inverse_x)
    inverse = exchange(mixed.reshape(SLABS, MROWS, 128))
    dec_wide = jnp.kron(jnp.eye(8, dtype=F32), dec_weight.T)
    out_wide = jnp.kron(jnp.eye(8, dtype=F32), out_weight[None, :])
    vm = pl.BlockSpec(memory_space=pltpu.VMEM)
    answers = pl.pallas_call(
        decode_kernel,
        out_shape=jax.ShapeDtypeStruct((SLOTS, PB), F32),
        in_specs=[SMEM] + [vm] * 11,
        out_specs=vm,
        scratch_shapes=[
            pltpu.VMEM((NY * 64, 128), F32),
            pltpu.VMEM((LINES * C, NZ), F32),
        ],
        compiler_params=params(),
        name="decode",
    )(
        tags,
        inverse.reshape(MY * MROWS, 128),
        base,
        got_queries.reshape(SLABS * QROWS, 128),
        *inverse_y,
        *inverse_z,
        *split_table(dec_wide),
        *split_table(out_wide),
    )
    returned = exchange(answers)
    return returned[route[4, 0:BLK]]


def solution(mesh):
    placed = (
        P(("geo", "slab"), None, None),
        P(("geo", "slab"), None, None),
        P(("geo", "slab"), None),
        P(("geo", "slab")),
        P(("geo", "slab"), None, None),
        P(("geo", "slab"), None),
        P(("geo", "slab")),
        P(None, "slab", None, None),
        P(),
        P(),
        P(),
        P(),
    )
    return jax.shard_map(
        local, mesh=mesh, in_specs=placed, out_specs=P(("geo", "slab"), None), check_vma=False
    )
```

time: 560 us -> 411 us (0.73)
  Pallas kernels: 0 us -> 149 us
  matrix products: 137 us -> 0 us
  other arithmetic: 83.4 us -> 4.63 us
  local copies, waits for them, and re-layouts: 93.1 us -> 15.6 us
  blocking collectives: 0 us -> 40 us
  starting transfers between devices: 63.2 us -> 31.8 us
  waiting for transfers between devices: 176 us -> 167 us
    pallas_call x0 -> x7, Pallas kernels: none -> 149 us  [the longest x1 56.6 us: local(): pl.pallas_call(decode_kernel, out_shape=jax.ShapeDtypeStruct((SLOTS, PB),...]
    dot_general x25 -> x0, matrix products: 137 us -> none  [the longest x22 72.7 us: einsum_exact(): return jnp.einsum(form, left, right, precision=lax.Precision.HIGHEST)]
    scatter-add x1 -> x0, other arithmetic: 54.2 us -> none  [local(): jax.ops.segment_sum(got_terms, target, num_segments=lines_dev + 1)]
    all_to_all x0 -> x1, blocking collectives: none -> 40 us  [local(): spectrum = exchange(message)]
    all_to_all x7 -> x4, starting transfers between devices: 63.2 us -> 31.8 us  [the longest x1 13 us: local(): got_queries = exchange(queries)]
    gather x6 -> x1, local copies, waits for them, and re-layouts: 20.7 us -> 1.24 us  [local(): return returned[route[4, 0:BLK]]]
    unnamed x1 -> x0, other arithmetic: 15 us -> none
    reshape x4 -> x2, local copies, waits for them, and re-layouts: 16.2 us -> 2.77 us  [the longest x1 1.38 us: local(): enc_line.reshape(BLK, 1)]
  transfers between devices with their start and end apart: 7 -> 4, of which waited for: 4 -> 4; matrix products, arithmetic and copies ran while one was open for 19% -> 2% of each run, Pallas kernels for 0% -> 8%
where the time goes in v1:
time: 411 us; the launch traced here: 409 us
  waiting for transfers between devices  167 us (41%)
  Pallas kernels  149 us (36%)
  blocking collectives  40 us (10%)
  starting transfers between devices  31.8 us (8%)
  local copies, waits for them, and re-layouts  15.6 us (4%)
  other arithmetic  4.63 us (1%)
    all_to_all x1, waiting for transfers between devices, local(): got_terms = exchange(packed)  140 us
    pallas_call x1, Pallas kernels, local(): pl.pallas_call(decode_kernel, out_shape=jax.ShapeDtypeStruct((SLOTS, PB),...  56.6 us
    all_to_all x1, blocking collectives, local(): spectrum = exchange(message)  40 us
    pallas_call x1, Pallas kernels, local(): pl.pallas_call(mix_kernel, out_shape=jax.ShapeDtypeStruct((SLABS * MROWS,...  28.4 us
    pallas_call x1, Pallas kernels, local(): pl.pallas_call(forward_kernel, out_shape=(jax.ShapeDtypeStruct((LINES * C...  24.9 us
    pallas_call x1, Pallas kernels, local(): pl.pallas_call(skip_kernel, out_shape=jax.ShapeDtypeStruct((LINES * C, NZ...  21.2 us
    all_to_all x1, starting transfers between devices, local(): got_queries = exchange(queries)  13 us
    pallas_call x1, Pallas kernels, local(): pl.pallas_call(encode_kernel, out_shape=jax.ShapeDtypeStruct((SLOTS, C, N...  12.2 us
  transfers between devices with their start and end apart: 4, of which 4 were waited for; matrix products, arithmetic and copies ran while one was open for 2% of the time, Pallas kernels for 8%

profile of v1, /device:TPU:1, one launch (start us, length us, event | category | flops | bytes accessed | tf_op | source)
XLA Modules:
  0.0 409.0 jit_solution(5483905272228558045)
XLA Ops:
  0.0 1.4 copy.48.ed_c
  1.4 1.4 copy.49.el_c
  2.8 1.4 copy.50.dd_c
  4.2 1.4 copy.51.dl_c
  5.5 1.8 copy.52.pos
  7.3 1.9 routes.1.route
  9.2 4.0 queries.1
  13.2 13.0 %all-to-all-start = ((f32[64,24,128]{2,1,0:T(8,128)}), f32[64,24,128]{2,1,0:T(8,128)S(1)}, u32[]{:S(2)}, u32[]{:S(2)}) async-start(f32[64,24,128]{2,1,0:T(8,128)} %queries.1), calls=%async_computation | async-start | bytes 1572864 | tf_op jit(solution)/shard_map/all_to_all | solution.py:401
  26.2 1.8 copy.54.pos
  28.0 12.2 %encode.1 = f32[384,32,128]{2,1,0:T(8,128)} custom-call(s32[8,384]{1,0:T(8,128)} %routes.1.route, f32[128,32,128]{2,1,0:T(8,128)} %feat.1, f32[128,3,128]{2,1,0:T(4,128)} %copy.54.pos), custom_call_target="tpu_custom_call" | custom-call | tf_op jit(solution)/shard_map/encode/pallas_call | solution.py:387
  40.2 9.0 %all-to-all-done = f32[64,24,128]{2,1,0:T(8,128)S(1)} async-done(((f32[64,24,128]{2,1,0:T(8,128)}), f32[64,24,128]{2,1,0:T(8,128)S(1)}, u32[]{:S(2)}, u32[]{:S(2)}) %all-to-all-start) | async-done | bytes 786464 | tf_op jit(solution)/shard_map/all_to_all | solution.py:401
  49.1 0.0 copy-start.1
  49.1 6.4 %all-to-all-start.1 = ((f32[384,32,128]{2,1,0:T(8,128)}), f32[384,32,128]{2,1,0:T(8,128)}, u32[]{:S(2)}, u32[]{:S(2)}) async-start(f32[384,32,128]{2,1,0:T(8,128)} %encode.1), calls=%async_computation.1 | async-start | bytes 12582912 | tf_op jit(solution)/shard_map/all_to_all | solution.py:402
  55.5 0.0 copy-done.1
  55.6 0.6 convert_bitcast_fusion.tags
  56.2 140.1 %all-to-all-done.1.got = f32[384,32,128]{2,1,0:T(8,128)} async-done(((f32[384,32,128]{2,1,0:T(8,128)}), f32[384,32,128]{2,1,0:T(8,128)}, u32[]{:S(2)}, u32[]{:S(2)}) %all-to-all-start.1) | async-done | bytes 6291488 | tf_op jit(solution)/shard_map/all_to_all | solution.py:402
  196.4 24.9 %forward.1 = (f32[8192,128]{1,0:T(8,128)}, f32[64,40,128]{2,1,0:T(8,128)}) custom-call(s32[64,12]{1,0:T(8,128)} %convert_bitcast_fusion.tags, f32[384,32,128]{2,1,0:T(8,128)} %all-to-all-done.1.got, bf16[128,128]{1,0:T(8,128)(2,1)} %constant.32.clone.dyh, bf16[128,128]{1,0:T(8,128)(2,1)} %constant.33.clone.dyl, bf16[256,128]{1,0:T(8,128)(2,1)} %constant.34.clone.zh, ...), custom_call_target="tpu_custom_call" | custom-call | tf_op jit(solution)/shard_map/forward/pallas_call | solution.py:404
  221.3 40.0 %all_to_all.32 = f32[64,40,128]{2,1,0:T(8,128)} all-to-all(f32[64,40,128]{2,1,0:T(8,128)} %get-tuple-element.7), channel_id=1, replica_groups=mesh['slab'=64,'geo'=4] {'slab'}, dimensions={0} | all-to-all | bytes 2621440 | tf_op jit(solution)/shard_map/all_to_all | solution.py:424
  261.3 0.0 copy-start.2
  261.3 0.0 copy-start.3
  261.3 28.4 %mix.1 = f32[2560,128]{1,0:T(8,128)} custom-call(f32[2560,128]{1,0:T(8,128)} %bitcast.28, bf16[33,64,2048]{2,1,0:T(8,128)(2,1)} %bitcast.26, bf16[256,64]{1,0:T(8,128)(2,1)} %constant.36.clone.xh, bf16[256,64]{1,0:T(8,128)(2,1)} %constant.37.clone.xl, bf16[128,2048]{1,0:T(8,128)(2,1)} %constant.38.clone.spread, bf16[256,128]{1,0:T(8,128)(2,1)} %constant.39.clone.gather, ...), custom_call_target="tpu_custom_call" | custom-call | tf_op jit(solution)/shard_map/mix/pallas_call | solution.py:441
  289.8 0.0 copy-start.4
  289.8 6.3 %all-to-all-start.3 = ((f32[64,40,128]{2,1,0:T(8,128)}), f32[64,40,128]{2,1,0:T(8,128)S(1)}, u32[]{:S(2)}, u32[]{:S(2)}) async-start(f32[64,40,128]{2,1,0:T(8,128)} %bitcast.27), calls=%async_computation.3 | async-start | bytes 2621440 | tf_op jit(solution)/shard_map/all_to_all | solution.py:459
  296.1 0.0 copy-done.2
  296.1 0.1 copy.55
  296.2 0.0 copy-done.3
  296.2 0.1 copy.57
  296.3 0.3 broadcast_multiply_fusion
  296.5 1.0 mul.73
  297.6 0.0 copy-done.4
  297.6 0.8 broadcast_in_dim_tile.4.bias
  298.4 0.3 mul.76
  298.7 0.1 mul.77
  298.7 0.1 mul.78
  298.8 0.0 copy-done.5
  298.8 0.1 mul.80
  298.9 0.6 fusion.2
  299.5 1.7 fusion
  301.2 0.7 fusion.1
  302.0 21.2 %skip.1.base = f32[8192,128]{1,0:T(8,128)} custom-call(bf16[256,256]{1,0:T(8,128)(2,1)} %get-tuple-element.12.kh, bf16[256,256]{1,0:T(8,128)(2,1)} %get-tuple-element.11.kl, f32[256,1]{1,0:T(8,128)} %broadcast_in_dim_tile.4.bias, f32[8192,128]{1,0:T(8,128)} %get-tuple-element.8.latent), custom_call_target="tpu_custom_call" | custom-call | tf_op jit(solution)/shard_map/skip/pallas_call | solution.py:426
  323.2 7.0 %all-to-all-done.3 = f32[64,40,128]{2,1,0:T(8,128)S(1)} async-done(((f32[64,40,128]{2,1,0:T(8,128)}), f32[64,40,128]{2,1,0:T(8,128)S(1)}, u32[]{:S(2)}, u32[]{:S(2)}) %all-to-all-start.3) | async-done | bytes 1310752 | tf_op jit(solution)/shard_map/all_to_all | solution.py:459
  330.2 1.1 copy-done
  331.3 56.6 %decode.1 = f32[384,128]{1,0:T(8,128)} custom-call(s32[64,12]{1,0:T(8,128)} %convert_bitcast_fusion.tags, f32[2560,128]{1,0:T(8,128)} %bitcast.29, f32[8192,128]{1,0:T(8,128)} %skip.1.base, f32[1536,128]{1,0:T(8,128)} %bitcast.30, bf16[256,64]{1,0:T(8,128)(2,1)} %constant.42.clone.yh, bf16[256,64]{1,0:T(8,128)(2,1)} %constant.43.clone.yl, ...), custom_call_target="tpu_custom_call" | custom-call | tf_op jit(solution)/shard_map/decode/pallas_call | solution.py:463
  388.0 1.7 all_to_all.24
  389.6 6.2 %all-to-all-start.4 = ((f32[64,6,128]{2,1,0:T(8,128)}), f32[64,6,128]{2,1,0:T(8,128)S(1)}, u32[]{:S(2)}, u32[]{:S(2)}) async-start(f32[64,6,128]{2,1,0:T(8,128)} %all_to_all.24), calls=%async_computation.4 | async-start | bytes 524288 | tf_op jit(solution)/shard_map/all_to_all | solution.py:484
  395.8 0.7 fusion.4
  396.5 11.3 %all-to-all-done.4 = f32[64,6,128]{2,1,0:T(8,128)S(1)} async-done(((f32[64,6,128]{2,1,0:T(8,128)}), f32[64,6,128]{2,1,0:T(8,128)S(1)}, u32[]{:S(2)}, u32[]{:S(2)}) %all-to-all-start.4) | async-done | bytes 196640 | tf_op jit(solution)/shard_map/all_to_all | solution.py:484
  407.8 1.2 gather_fusion
  (8 shorter events, 0.1 us)
Async XLA Ops:
  13.2 35.9 %all-to-all-start = ((f32[64,24,128]{2,1,0:T(8,128)}), f32[64,24,128]{2,1,0:T(8,128)S(1)}, u32[]{:S(2)}, u32[]{:S(2)}) async-start(f32[64,24,128]{2,1,0:T(8,128)} %queries.1), calls=%async_computation | async-start | bytes 1572864 | tf_op jit(solution)/shard_map/all_to_all | solution.py:401
  49.1 6.4 %copy-start.1 = (f32[64,24,128]{2,1,0:T(8,128)}, f32[64,24,128]{2,1,0:T(8,128)S(1)}, u32[]{:S(2)}) copy-start(f32[64,24,128]{2,1,0:T(8,128)S(1)} %all-to-all-done) | copy-start | bytes 2359300
  49.1 147.2 %all-to-all-start.1 = ((f32[384,32,128]{2,1,0:T(8,128)}), f32[384,32,128]{2,1,0:T(8,128)}, u32[]{:S(2)}, u32[]{:S(2)}) async-start(f32[384,32,128]{2,1,0:T(8,128)} %encode.1), calls=%async_computation.1 | async-start | bytes 12582912 | tf_op jit(solution)/shard_map/all_to_all | solution.py:402
  261.3 34.8 %copy-start.2 = (f32[32,32]{1,0:T(8,128)S(1)}, f32[32,32]{1,0:T(8,128)}, u32[]{:S(2)}) copy-start(f32[32,32]{1,0:T(8,128)} %param.34) | copy-start | bytes 12292
  261.3 34.8 %copy-start.3 = (f32[32,32]{1,0:T(8,128)S(1)}, f32[32,32]{1,0:T(8,128)}, u32[]{:S(2)}) copy-start(f32[32,32]{1,0:T(8,128)} %param.36) | copy-start | bytes 12292
  289.8 7.8 %copy-start.4 = (f32[32]{0:T(128)S(1)}, f32[32]{0:T(128)}, u32[]{:S(2)}) copy-start(f32[32]{0:T(128)} %param.35) | copy-start | bytes 388
  289.8 9.0 %copy-start.5 = (f32[32]{0:T(128)S(1)}, f32[32]{0:T(128)}, u32[]{:S(2)}) copy-start(f32[32]{0:T(128)} %param.37) | copy-start | bytes 388
  289.8 40.5 %all-to-all-start.3 = ((f32[64,40,128]{2,1,0:T(8,128)}), f32[64,40,128]{2,1,0:T(8,128)S(1)}, u32[]{:S(2)}, u32[]{:S(2)}) async-start(f32[64,40,128]{2,1,0:T(8,128)} %bitcast.27), calls=%async_computation.3 | async-start | bytes 2621440 | tf_op jit(solution)/shard_map/all_to_all | solution.py:459
  330.2 1.1 copy-start
  389.6 18.1 %all-to-all-start.4 = ((f32[64,6,128]{2,1,0:T(8,128)}), f32[64,6,128]{2,1,0:T(8,128)S(1)}, u32[]{:S(2)}, u32[]{:S(2)}) async-start(f32[64,6,128]{2,1,0:T(8,128)} %all_to_all.24), calls=%async_computation.4 | async-start | bytes 524288 | tf_op jit(solution)/shard_map/all_to_all | solution.py:484

commit v2 on v1

v2 whole, which is shorter than its diff:
```python
import functools
import math

import jax
import jax.numpy as jnp
import numpy as np
from jax import lax
from jax.experimental import pallas as pl
from jax.experimental.pallas import tpu as pltpu
from jax.sharding import PartitionSpec as P

C = 32
NX = 128
NY = 128
NZ = 128
MX = 64
MY = 64
MZ = 33
PB = 128
BLK = 128
SLABS = 64
PLANES = NX // SLABS
CAP = 6
SLOTS = SLABS * CAP
LINES = PLANES * NY
MROWS = 40
QROWS = 24
VMEM_LIMIT = 60 * 1024 * 1024

radius_scale = 0.7
spread_cells = 1.5
BF = jnp.bfloat16
F32 = jnp.float32


def split_np(table):
    table = np.asarray(table, np.float32)
    high = table.astype(jnp.bfloat16)
    low = (table - high.astype(np.float32)).astype(jnp.bfloat16)
    return high, low


def left_np(table):
    high, low = split_np(table)
    return np.concatenate([high, low, high], axis=1)


def right_np(table):
    high, low = split_np(table)
    return np.concatenate([high, high, low], axis=0)


def split(values):
    high = values.astype(BF)
    low = (values - high.astype(F32)).astype(BF)
    return high, low


def left_table(values):
    high = lax.reduce_precision(values, 8, 7)
    low = (values - high).astype(BF)
    high = high.astype(BF)
    return jnp.concatenate([high, low, high], axis=1)


def left3(values):
    high, low = split(values)
    return jnp.concatenate([high, low, high], axis=1)


def right3(values):
    high, low = split(values)
    return jnp.concatenate([high, high, low], axis=0)


def mm(left, right):
    return jnp.dot(left, right, preferred_element_type=F32)


def nt(left, right):
    return lax.dot_general(left, right, (((1,), (1,)), ((), ())), preferred_element_type=F32)


def kept(length, count):
    counter = np.arange(count)
    return np.where(counter < count // 2, counter, counter + length - count)


def tables():
    cells = np.arange(NY)
    ky = kept(NY, MY)
    angle = 2.0 * math.pi * ((ky[:, None] * cells[None, :]) % NY) / NY
    cos_y, sin_y = np.cos(angle), np.sin(angle)
    forward_y = np.concatenate([cos_y, -sin_y], axis=0)
    inverse_y = np.concatenate([cos_y.T, sin_y.T], axis=0) / NY
    z_angle = 2.0 * math.pi * ((np.arange(NZ)[:, None] * np.arange(MZ)[None, :]) % NZ) / NZ
    cos_z, sin_z = np.cos(z_angle), np.sin(z_angle)
    forward_z = np.zeros((2 * NZ, 128))
    forward_z[:NZ, :MZ] = cos_z
    forward_z[:NZ, 64 : 64 + MZ] = -sin_z
    forward_z[NZ:, :MZ] = sin_z
    forward_z[NZ:, 64 : 64 + MZ] = cos_z
    weight = np.where(np.arange(MZ) == 0, 1.0, 2.0) / NZ
    inverse_z = np.zeros((2, 2, 64, 2, NZ))
    for twin in range(2):
        inverse_z[0, twin, :MZ, twin, :] = (cos_z * weight[None, :]).T
        inverse_z[1, twin, :MZ, twin, :] = -(sin_z * weight[None, :]).T
    inverse_z = inverse_z.reshape(256, 256)
    kx = kept(NX, MX)
    owner = np.arange(SLABS)
    forward_x, inverse_x = [], []
    for part in (np.cos, np.sin):
        for plane in range(PLANES):
            turns = (kx[:, None] * (PLANES * owner + plane)[None, :]) % NX
            table = part(2.0 * math.pi * turns / NX)
            forward_x.append(table)
            inverse_x.append(table.T / NX)
    forward_x = np.concatenate(forward_x, axis=0)
    inverse_x = np.concatenate(inverse_x, axis=0)
    spread = np.zeros((2, PLANES, C, 2, C, C))
    for channel in range(C):
        for part in range(2):
            spread[part, :, channel, part, channel, :] = 1.0
    spread = spread.reshape(128, 2 * C * C)
    gather = np.zeros((2, 4, C, 2, PLANES, C))
    for channel in range(C):
        for part in range(2):
            gather[part, :, channel, part, :, channel] = 1.0
    gather = gather.reshape(256, 128)
    return (
        left_np(forward_y),
        left_np(inverse_y),
        right_np(forward_z),
        right_np(inverse_z),
        left_np(forward_x),
        left_np(inverse_x),
        np.asarray(np.concatenate([spread, spread], axis=0), jnp.bfloat16),
        np.asarray(np.concatenate([gather, gather], axis=0), jnp.bfloat16),
    )


def params(**extra):
    return pltpu.CompilerParams(vmem_limit_bytes=VMEM_LIMIT, **extra)


def cost(microseconds):
    return pl.CostEstimate(
        flops=0, transcendentals=0, bytes_accessed=int(microseconds * 2_000_000)
    )


def whole(shape):
    return pl.BlockSpec(shape, lambda *_: (0,) * len(shape))


SMEM = pl.BlockSpec(memory_space=pltpu.SMEM)


def routes_kernel(ed, el, dd, dl, out):
    rows = lax.broadcasted_iota(jnp.int32, (BLK, BLK), 0)
    cols = lax.broadcasted_iota(jnp.int32, (BLK, BLK), 1)

    def column(row):
        spread_row = jnp.broadcast_to(row.astype(F32), (BLK, BLK))
        return jnp.sum(jnp.where(rows == cols, spread_row, 0.0), axis=1, keepdims=True)

    def one(dest_r, line_r):
        dest_c = column(dest_r).astype(jnp.int32)
        line_c = column(line_r)
        same = dest_c == dest_r
        before_r = jnp.sum(jnp.where(same & (rows < cols), 1.0, 0.0), axis=0, keepdims=True)
        slot_r = dest_r * CAP + before_r.astype(jnp.int32)
        slot_c = column(slot_r).astype(jnp.int32)
        match = slot_c == lax.broadcasted_iota(jnp.int32, (BLK, SLOTS), 1)
        number = lax.broadcasted_iota(jnp.int32, (BLK, SLOTS), 0).astype(F32)
        filled = jnp.sum(jnp.where(match, 1.0, 0.0), axis=0, keepdims=True)
        source = jnp.sum(jnp.where(match, number, 0.0), axis=0, keepdims=True)
        line = jnp.sum(jnp.where(match, line_c, 0.0), axis=0, keepdims=True)
        return slot_r, filled, source.astype(jnp.int32), line.astype(jnp.int32)

    out[...] = jnp.zeros((8, SLOTS), jnp.int32)
    _, filled, source, line = one(ed[...], el[...])
    out[0:1, :] = jnp.where(filled > 0.5, source, BLK)
    out[1:2, :] = line
    slot, _, source, line = one(dd[...], dl[...])
    out[2:3, :] = source
    out[3:4, :] = line
    out[4:5, 0:BLK] = slot


def encode_kernel(route, feat, pos, out, terms):
    step = pl.program_id(0)

    @pl.when(step == 0)
    def _():
        terms[BLK] = jnp.zeros((C, NZ), F32)

    @pl.when(step < 8)
    def _():
        grid_cells = lax.broadcasted_iota(jnp.int32, (NZ, PB), 0).astype(F32)
        for b in range(16):
            a, o, t = pos[0, b : b + 1, :], pos[1, b : b + 1, :], pos[2, b : b + 1, :]
            radial = jnp.exp((a * a + o * o) * (-1.0 / (2.0 * radius_scale**2)))
            offset = grid_cells - (t + 1.0) * (0.5 * (NZ - 1))
            rows = jnp.exp(offset * offset * (-1.0 / (2.0 * spread_cells**2)))
            fh, fl = split(feat[b] * radial)
            kh, kl = split(rows)
            both = nt(jnp.concatenate([fh, fl], axis=0), kh)
            terms[step * 16 + b] = both[:C] + (both[C:] + nt(fh, kl))

    @pl.when(step >= 8)
    def _():
        base = (step - 8) * 48

        def put(i, carry):
            out[i] = terms[route[0, base + i]]
            return carry

        lax.fori_loop(0, 48, put, 0, unroll=8)


def queries_kernel(route, pos, out):
    lane = lax.broadcasted_iota(jnp.int32, (1, 128), 1)

    def peer(d, carry):
        tags = jnp.zeros((1, 128), F32)
        for r in range(CAP):
            s = d * CAP + r
            for part in range(3):
                out[d, 3 * r + part : 3 * r + part + 1, :] = pos[part, pl.ds(route[2, s], 1), :]
            tags = jnp.where(lane == r, route[3, s].astype(F32), tags)
            tags = jnp.where(lane == CAP + r, route[1, s].astype(F32), tags)
        out[d, 18:19, :] = tags
        out[d, 19:24, :] = jnp.zeros((5, 128), F32)
        return carry

    lax.fori_loop(0, SLABS, peer, 0)


def profile_kernel(pos, out):
    step = pl.program_id(0)
    grid_cells = lax.broadcasted_iota(jnp.int32, (NZ, PB), 0).astype(F32)

    def one(d, carry):
        for r in range(CAP):
            a = pos[d, 3 * r : 3 * r + 1, :]
            o = pos[d, 3 * r + 1 : 3 * r + 2, :]
            t = pos[d, 3 * r + 2 : 3 * r + 3, :]
            radial = jnp.exp((a * a + o * o) * (-1.0 / (2.0 * radius_scale**2)))
            offset = grid_cells - (t + 1.0) * (0.5 * (NZ - 1))
            rows = jnp.exp(offset * offset * (-1.0 / (2.0 * spread_cells**2))) * radial
            kh, kl = split(rows)
            out[d * CAP + r, :, 0:PB] = kh
            out[d * CAP + r, :, PB : 2 * PB] = kl
        return carry

    lax.fori_loop(0, 4, one, 0)


def forward_kernel(tags, got, dy, fz, latent, message, scratch):
    step = pl.program_id(0)

    @pl.when(step == 0)
    def _():
        latent[...] = jnp.zeros_like(latent)

    for q in range(8):
        for r in range(CAP):
            line = tags[step * 8 + q, CAP + r]
            start = pl.multiple_of(line * C, C)
            latent[pl.ds(start, C), :] += got[q * CAP + r]

    @pl.when(step == 7)
    def _():
        def quad(i, carry):
            plane = i // (C // 4)
            channel = (i % (C // 4)) * 4
            start = plane * NY * C + channel
            data = jnp.concatenate(
                [latent[pl.ds(start + n, NY, stride=C), :] for n in range(4)], axis=1
            )
            y = mm(dy[...], right3(data))
            x = jnp.concatenate(
                [
                    jnp.concatenate(
                        [y[:MY, n * NZ : n * NZ + NZ], y[MY:, n * NZ : n * NZ + NZ]], axis=1
                    )
                    for n in range(4)
                ],
                axis=0,
            )
            at = pl.multiple_of((plane * C + channel) * MY, MY)
            scratch[pl.ds(at, 4 * MY), :] = mm(left3(x), fz[...])
            return carry

        lax.fori_loop(0, PLANES * C // 4, quad, 0, unroll=2)

        def flip(j, carry):
            turned = jnp.transpose(scratch[pl.ds(j, PLANES * C, stride=MY), :])
            message[j, :, 0:64] = turned[:MROWS]
            message[j, :, 64:128] = turned[64 : 64 + MROWS]
            return carry

        lax.fori_loop(0, MY, flip, 0, unroll=4)


def skip_kernel(kron, bias, latent, out):
    for n in range(4):
        rows = slice(n * 256, n * 256 + 256)
        out[rows, :] = mm(kron[...], right3(latent[rows, :])) + bias[...]


def planes_of(t, first_plane):
    u = jnp.where(first_plane, t[0:64], t[64:128])
    w = jnp.where(first_plane, t[128:192], t[192:256])
    return u, pltpu.roll(w, 64, 1)


def mix_kernel(spec, weight, fx, spread, gather, ix, out):
    step = pl.program_id(0)
    lane = lax.broadcasted_iota(jnp.int32, (64, 128), 1)
    first_plane = (lane & 32) == 0
    real_part = lane < 64
    data = jnp.concatenate(
        [spec[pl.ds(step * 3 + n, SLABS, stride=MROWS), :] for n in range(3)], axis=1
    )
    t = mm(fx[...], right3(data))
    rows = []
    for n in range(3):
        u, w = planes_of(t[:, n * 128 : n * 128 + 128], first_plane)
        rows.append(u + jnp.where(real_part, w, -w))
    sh, sl = split(jnp.concatenate(rows, axis=0))
    wide = mm(jnp.concatenate([sh, sl], axis=1), spread[...])
    rows = []
    for n in range(3):
        acc_re = jnp.zeros((64, 128), F32)
        acc_im = jnp.zeros((64, 128), F32)
        part = slice(n * 64, n * 64 + 64)
        for piece in range(8):
            re = slice(piece * 128, piece * 128 + 128)
            im = slice(C * C + piece * 128, C * C + piece * 128 + 128)
            w_re = weight[n, :, re].astype(F32)
            w_im = weight[n, :, im].astype(F32)
            acc_re += wide[part, re] * w_re - wide[part, im] * w_im
            acc_im += wide[part, re] * w_im + wide[part, im] * w_re
        rows.append(jnp.concatenate([acc_re, acc_im], axis=1))
    ah, al = split(jnp.concatenate(rows, axis=0))
    o = mm(jnp.concatenate([ah, al], axis=1), gather[...])
    data = jnp.concatenate([o[n * 64 : n * 64 + 64] for n in range(3)], axis=1)
    t = mm(ix[...], right3(data))
    for n in range(3):
        u, w = planes_of(t[:, n * 128 : n * 128 + 128], first_plane)
        out[pl.ds(step * 3 + n, SLABS, stride=MROWS), :] = u + jnp.where(real_part, -w, w)


def decode_kernel(tags, inverse, base, profile, iy, iz, dw, ow, out, modes, hidden):
    step = pl.program_id(0)

    @pl.when(step == 0)
    def _():
        lane = lax.broadcasted_iota(jnp.int32, (NY, 128), 1)
        real_part = lane < 64

        def clear(n, carry):
            modes[pl.ds(pl.multiple_of(n * 64 + 32, 32), 32), :] = jnp.zeros((32, 128), F32)
            return carry

        lax.fori_loop(0, NY, clear, 0, unroll=8)

        def planes(i, carry):
            data = jnp.concatenate(
                [inverse[pl.ds(i * 3 + n, MY, stride=MROWS), :] for n in range(3)], axis=1
            )
            t = mm(iy[...], right3(data))
            for n in range(3):
                cols = slice(n * 128, n * 128 + 128)
                w = pltpu.roll(t[NY:, cols], 64, 1)
                modes[pl.ds(i * 3 + n, NY, stride=64), :] = t[:NY, cols] + jnp.where(
                    real_part, -w, w
                )
            return carry

        lax.fori_loop(0, MZ // 3, planes, 0)

        def columns(i, carry):
            rows = []
            for n in range(4):
                at = pl.multiple_of((i * 4 + n) * 128, 128)
                turned = jnp.transpose(modes[pl.ds(at, 128), :])
                rows.append(jnp.concatenate([turned[:64], turned[64:]], axis=1))
            s = mm(left3(jnp.concatenate(rows, axis=0)), iz[...])
            for n in range(4):
                for plane in range(PLANES):
                    for twin in range(2):
                        at = pl.multiple_of((plane * NY + 2 * (i * 4 + n) + twin) * C, C)
                        top = n * 64 + plane * C
                        value = s[top : top + C, twin * NZ : twin * NZ + NZ] + base[pl.ds(at, C), :]
                        hidden[pl.ds(at, C), :] = jax.nn.gelu(value)
            return carry

        lax.fori_loop(0, NY // 8, columns, 0)

    for pair in range(2):
        sides = []
        for half in range(2):
            near = []
            for i in range(6):
                q = (pair * 2 + half) * 6 + i
                line = tags[step * 4 + pair * 2 + half, i]
                hh, hl = split(hidden[pl.ds(pl.multiple_of(line * C, C), C), :])
                both = mm(jnp.concatenate([hh, hl], axis=0), profile[q])
                near.append(both[:C, :PB] + (both[C:, :PB] + both[:C, PB:]))
            sides.append(jnp.concatenate(near, axis=0))
        act = jax.nn.gelu(mm(dw[...], right3(jnp.concatenate(sides, axis=1))))
        result = mm(ow[...], right3(act))
        for half in range(2):
            d = pair * 2 + half
            out[d] = result[:, half * PB : half * PB + PB]


def local(
    enc_feat,
    enc_pos,
    enc_dest,
    enc_line,
    dec_pos,
    dec_dest,
    dec_line,
    mode_weight,
    skip_weight,
    skip_bias,
    dec_weight,
    out_weight,
):
    forward_y, inverse_y, forward_z, inverse_z, forward_x, inverse_x, spread, gather = tables()
    exchange = functools.partial(
        lax.all_to_all, axis_name="slab", split_axis=0, concat_axis=0, tiled=True
    )
    route = pl.pallas_call(
        routes_kernel, out_shape=jax.ShapeDtypeStruct((8, SLOTS), jnp.int32), name="routes"
    )(
        enc_dest.reshape(1, BLK),
        enc_line.reshape(1, BLK),
        dec_dest.reshape(1, BLK),
        dec_line.reshape(1, BLK),
    )
    queries = pl.pallas_call(
        queries_kernel,
        out_shape=jax.ShapeDtypeStruct((SLABS, QROWS, 128), F32),
        in_specs=[SMEM, whole((3, BLK, PB))],
        out_specs=whole((SLABS, QROWS, 128)),
        name="queries",
    )(route, jnp.transpose(dec_pos, (1, 0, 2)))
    packed = pl.pallas_call(
        encode_kernel,
        out_shape=jax.ShapeDtypeStruct((SLOTS, C, NZ), F32),
        grid=(16,),
        in_specs=[
            SMEM,
            pl.BlockSpec((16, C, PB), lambda i: (jnp.minimum(i, 7), 0, 0)),
            pl.BlockSpec((3, 16, PB), lambda i: (0, jnp.minimum(i, 7), 0)),
        ],
        out_specs=pl.BlockSpec((48, C, NZ), lambda i: (jnp.maximum(i - 8, 0), 0, 0)),
        scratch_shapes=[pltpu.VMEM((BLK + 1, C, NZ), F32)],
        compiler_params=params(),
        cost_estimate=cost(12),
        name="encode",
    )(route, enc_feat, jnp.transpose(enc_pos, (1, 0, 2)))
    got_queries = exchange(queries)
    got_terms = exchange(packed)
    tags = got_queries[:, 18, 0 : 2 * CAP].astype(jnp.int32)
    profile = pl.pallas_call(
        profile_kernel,
        out_shape=jax.ShapeDtypeStruct((SLOTS, NZ, 2 * PB), BF),
        grid=(16,),
        in_specs=[pl.BlockSpec((4, QROWS, PB), lambda i: (i, 0, 0))],
        out_specs=pl.BlockSpec((24, NZ, 2 * PB), lambda i: (i, 0, 0)),
        compiler_params=params(),
        cost_estimate=cost(25),
        name="profile",
    )(got_queries)
    skip_wide = left_table(jnp.kron(jnp.eye(8, dtype=F32), skip_weight.T))
    skip_bias_wide = jnp.tile(skip_bias, 8)[:, None]
    dec_wide = left_table(jnp.kron(jnp.eye(CAP, dtype=F32), dec_weight.T))
    out_wide = left_table(jnp.kron(jnp.eye(CAP, dtype=F32), out_weight[None, :]))
    latent, message = pl.pallas_call(
        forward_kernel,
        out_shape=(
            jax.ShapeDtypeStruct((LINES * C, NZ), F32),
            jax.ShapeDtypeStruct((MY, MROWS, 128), F32),
        ),
        grid=(8,),
        in_specs=[
            SMEM,
            pl.BlockSpec((48, C, NZ), lambda i: (i, 0, 0)),
            whole((2 * MY, 3 * NY)),
            whole((6 * NZ, 128)),
        ],
        out_specs=(whole((LINES * C, NZ)), whole((MY, MROWS, 128))),
        scratch_shapes=[pltpu.VMEM((PLANES * C * MY, 128), F32)],
        compiler_params=params(),
        name="forward",
    )(tags, got_terms, forward_y, forward_z)
    spectrum = exchange(message)
    base = pl.pallas_call(
        skip_kernel,
        out_shape=jax.ShapeDtypeStruct((LINES * C, NZ), F32),
        grid=(8,),
        in_specs=[
            whole((256, 768)),
            whole((256, 1)),
            pl.BlockSpec((1024, NZ), lambda i: (i, 0)),
        ],
        out_specs=pl.BlockSpec((1024, NZ), lambda i: (i, 0)),
        compiler_params=params(),
        cost_estimate=cost(12),
        name="skip",
    )(skip_wide, skip_bias_wide, latent)
    weight = jnp.transpose(mode_weight.reshape(MX, MZ, 2 * C * C), (1, 0, 2))
    mixed = pl.pallas_call(
        mix_kernel,
        out_shape=jax.ShapeDtypeStruct((SLABS * MROWS, 128), F32),
        grid=(11,),
        in_specs=[
            whole((SLABS * MROWS, 128)),
            pl.BlockSpec((3, MX, 2 * C * C), lambda i: (i, 0, 0)),
            whole((256, 192)),
            whole((256, 2 * C * C)),
            whole((512, 128)),
            whole((256, 192)),
        ],
        out_specs=whole((SLABS * MROWS, 128)),
        compiler_params=params(),
        name="mix",
    )(spectrum.reshape(SLABS * MROWS, 128), weight, forward_x, spread, gather, inverse_x)
    inverse = exchange(mixed.reshape(SLABS, MROWS, 128))
    answers = pl.pallas_call(
        decode_kernel,
        out_shape=jax.ShapeDtypeStruct((SLABS, CAP, PB), F32),
        grid=(16,),
        in_specs=[
            SMEM,
            whole((MY * MROWS, 128)),
            whole((LINES * C, NZ)),
            pl.BlockSpec((24, NZ, 2 * PB), lambda i: (i, 0, 0)),
            whole((2 * NY, 192)),
            whole((768, 2 * NZ)),
            whole((CAP * C, 3 * CAP * C)),
            whole((CAP, 3 * CAP * C)),
        ],
        out_specs=pl.BlockSpec((4, CAP, PB), lambda i: (i, 0, 0)),
        scratch_shapes=[
            pltpu.VMEM((NY * 64, 128), F32),
            pltpu.VMEM((LINES * C, NZ), F32),
        ],
        compiler_params=params(),
        name="decode",
    )(
        tags,
        inverse.reshape(MY * MROWS, 128),
        base,
        profile,
        inverse_y,
        inverse_z,
        dec_wide,
        out_wide,
    )
    returned = exchange(answers)
    slot = route[4, 0:BLK]
    return returned[slot // CAP, slot % CAP]


def solution(mesh):
    placed = (
        P(("geo", "slab"), None, None),
        P(("geo", "slab"), None, None),
        P(("geo", "slab"), None),
        P(("geo", "slab")),
        P(("geo", "slab"), None, None),
        P(("geo", "slab"), None),
        P(("geo", "slab")),
        P(None, "slab", None, None),
        P(),
        P(),
        P(),
        P(),
    )
    return jax.shard_map(
        local, mesh=mesh, in_specs=placed, out_specs=P(("geo", "slab"), None), check_vma=False
    )
```

time: 411 us -> 367 us (0.89)
  Pallas kernels: 149 us -> 117 us
  local copies, waits for them, and re-layouts: 15.6 us -> 4.72 us
    pallas_call x1, Pallas kernels: 21.2 us -> 8.75 us  [local(): pl.pallas_call(skip_kernel, out_shape=jax.ShapeDtypeStruct((LINES * C, NZ...]
    pallas_call x1, Pallas kernels: 28.4 us -> 17.1 us  [local(): pl.pallas_call(mix_kernel, out_shape=jax.ShapeDtypeStruct((SLABS * MROWS,...]
    unnamed x16 -> x12, local copies, waits for them, and re-layouts: 7.42 us -> 1.16 us
    pallas_call x1, Pallas kernels: 24.9 us -> 20.6 us  [local(): pl.pallas_call(forward_kernel, out_shape=(jax.ShapeDtypeStruct((LINES * C...]
    pallas_call x1 -> x2, Pallas kernels: 56.6 us -> 52.5 us  [the longest x1 36.7 us: local(): pl.pallas_call(decode_kernel, out_shape=jax.ShapeDtypeStruct((SLABS, CAP,...]
  transfers between devices with their start and end apart: 4 -> 4, of which waited for: 4 -> 4; matrix products, arithmetic and copies ran while one was open for 2% -> 2% of each run, Pallas kernels for 8% -> 10%
where the time goes in v2:
time: 367 us; the launch traced here: 365 us
  waiting for transfers between devices  167 us (46%)
  Pallas kernels  117 us (32%)
  blocking collectives  39.9 us (11%)
  starting transfers between devices  31.8 us (9%)
  local copies, waits for them, and re-layouts  4.72 us (1%)
  other arithmetic  3.9 us (1%)
    all_to_all x1, waiting for transfers between devices, local(): got_terms = exchange(packed)  140 us
    all_to_all x1, blocking collectives, local(): spectrum = exchange(message)  39.9 us
    pallas_call x1, Pallas kernels, local(): pl.pallas_call(decode_kernel, out_shape=jax.ShapeDtypeStruct((SLABS, CAP,...  36.7 us
    pallas_call x1, Pallas kernels, local(): pl.pallas_call(forward_kernel, out_shape=(jax.ShapeDtypeStruct((LINES * C...  20.6 us
    pallas_call x1, Pallas kernels, local(): pl.pallas_call(mix_kernel, out_shape=jax.ShapeDtypeStruct((SLABS * MROWS,...  17.1 us
    pallas_call x1, Pallas kernels, local(): pl.pallas_call(profile_kernel, out_shape=jax.ShapeDtypeStruct((SLOTS, NZ,...  15.8 us
    all_to_all x1, starting transfers between devices, local(): got_queries = exchange(queries)  13 us
    pallas_call x1, Pallas kernels, local(): pl.pallas_call(encode_kernel, out_shape=jax.ShapeDtypeStruct((SLOTS, C, N...  12.3 us
  transfers between devices with their start and end apart: 4, of which 4 were waited for; matrix products, arithmetic and copies ran while one was open for 2% of the time, Pallas kernels for 10%

profile of v2, /device:TPU:1, one launch (start us, length us, event | category | flops | bytes accessed | tf_op | source)
XLA Modules:
  0.0 364.9 jit_solution(1532484422845061397)
XLA Ops:
  0.0 1.6 routes.1.route
  1.6 4.2 %queries.1 = f32[64,24,128]{2,1,0:T(8,128)} custom-call(s32[8,384]{1,0:T(8,128)} %routes.1.route, f32[3,128,128]{2,1,0:T(8,128)} %bitcast.43), custom_call_target="tpu_custom_call" | custom-call | tf_op jit(solution)/shard_map/queries/pallas_call | solution.py:447
  5.8 13.0 %all-to-all-start = ((f32[64,24,128]{2,1,0:T(8,128)}), f32[64,24,128]{2,1,0:T(8,128)S(1)}, u32[]{:S(2)}, u32[]{:S(2)}) async-start(f32[64,24,128]{2,1,0:T(8,128)} %queries.1), calls=%async_computation | async-start | bytes 1572864 | tf_op jit(solution)/shard_map/all_to_all | solution.py:469
  18.8 12.3 %encode.1 = f32[384,32,128]{2,1,0:T(8,128)} custom-call(s32[8,384]{1,0:T(8,128)} %routes.1.route, f32[128,32,128]{2,1,0:T(8,128)} %feat.1, f32[3,128,128]{2,1,0:T(8,128)} %bitcast.44), custom_call_target="tpu_custom_call" | custom-call | bytes 24000000 | tf_op jit(solution)/shard_map/encode/pallas_call | solution.py:454
  31.1 10.6 %all-to-all-done.pos = f32[64,24,128]{2,1,0:T(8,128)S(1)} async-done(((f32[64,24,128]{2,1,0:T(8,128)}), f32[64,24,128]{2,1,0:T(8,128)S(1)}, u32[]{:S(2)}, u32[]{:S(2)}) %all-to-all-start) | async-done | bytes 786464 | tf_op jit(solution)/shard_map/all_to_all | solution.py:469
  41.8 0.0 copy-start.1
  41.8 6.4 %all-to-all-start.1 = ((f32[384,32,128]{2,1,0:T(8,128)}), f32[384,32,128]{2,1,0:T(8,128)}, u32[]{:S(2)}, u32[]{:S(2)}) async-start(f32[384,32,128]{2,1,0:T(8,128)} %encode.1), calls=%async_computation.1 | async-start | bytes 12582912 | tf_op jit(solution)/shard_map/all_to_all | solution.py:470
  48.1 0.0 copy-done.1
  48.2 0.6 convert_bitcast_fusion.tags
  48.8 140.1 %all-to-all-done.1.got = f32[384,32,128]{2,1,0:T(8,128)} async-done(((f32[384,32,128]{2,1,0:T(8,128)}), f32[384,32,128]{2,1,0:T(8,128)}, u32[]{:S(2)}, u32[]{:S(2)}) %all-to-all-start.1) | async-done | bytes 6291488 | tf_op jit(solution)/shard_map/all_to_all | solution.py:470
  189.0 20.6 %forward.1 = (f32[8192,128]{1,0:T(8,128)}, f32[64,40,128]{2,1,0:T(8,128)}) custom-call(s32[64,12]{1,0:T(8,128)} %convert_bitcast_fusion.tags, f32[384,32,128]{2,1,0:T(8,128)} %all-to-all-done.1.got, bf16[128,384]{1,0:T(8,128)(2,1)} %constant.40.clone.dy, bf16[768,128]{1,0:T(8,128)(2,1)} %constant.41.clone.fz), custom_call_target="tpu_custom_call" | custom-call | tf_op jit(solution)/shard_map/forward/pallas_call | solution.py:486
  209.6 39.9 %all_to_all.25 = f32[64,40,128]{2,1,0:T(8,128)} all-to-all(f32[64,40,128]{2,1,0:T(8,128)} %get-tuple-element.7), channel_id=1, replica_groups=mesh['slab'=64,'geo'=4] {'slab'}, dimensions={0} | all-to-all | bytes 2621440 | tf_op jit(solution)/shard_map/all_to_all | solution.py:504
  249.5 0.0 copy-start.2
  249.5 17.1 %mix.1 = f32[2560,128]{1,0:T(8,128)} custom-call(f32[2560,128]{1,0:T(8,128)} %bitcast.42, bf16[33,64,2048]{2,1,0:T(8,128)(2,1)} %bitcast.39, bf16[256,192]{1,0:T(8,128)(2,1)} %constant.42.clone.fx, bf16[256,2048]{1,0:T(8,128)(2,1)} %constant.43.clone.spread, bf16[512,128]{1,0:T(8,128)(2,1)} %constant.44.clone.gather, bf16[256,192]{1,0:T(8,128)(2,1)} %constant.45.clone.ix), custom_call_target="tpu_custom_call" | custom-call | tf_op jit(solution)/shard_map/mix/pallas_call | solution.py:520
  266.6 0.0 copy-start.4
  266.6 0.0 copy-start.3
  266.6 0.0 copy-start.5
  266.6 6.3 %all-to-all-start.3 = ((f32[64,40,128]{2,1,0:T(8,128)}), f32[64,40,128]{2,1,0:T(8,128)S(1)}, u32[]{:S(2)}, u32[]{:S(2)}) async-start(f32[64,40,128]{2,1,0:T(8,128)} %bitcast.41), calls=%async_computation.3 | async-start | bytes 2621440 | tf_op jit(solution)/shard_map/all_to_all | solution.py:536
  272.9 0.0 copy-done.2
  272.9 0.1 copy.33
  273.0 0.1 broadcast_multiply_fusion
  273.1 0.3 mul.80
  273.5 0.0 copy-done.4
  273.5 0.8 broadcast_in_dim_tile.4.bias
  274.3 0.0 copy-done.3
  274.3 0.1 copy.35
  274.3 0.1 broadcast_multiply_fusion.1
  274.5 0.2 mul.84
  274.7 0.1 mul.85
  274.7 0.1 mul.86
  274.8 0.0 copy-done.5
  274.8 0.1 mul.88
  274.9 0.7 pad_maximum_fusion.2.ow
  275.6 0.8 pad_maximum_fusion.1.dw
  276.5 0.8 pad_maximum_fusion.kron
  277.2 15.8 %profile.1 = bf16[384,128,256]{2,1,0:T(8,128)(2,1)} custom-call(f32[64,24,128]{2,1,0:T(8,128)} %copy-done.1), custom_call_target="tpu_custom_call" | custom-call | bytes 50000000 | tf_op jit(solution)/shard_map/profile/pallas_call | solution.py:472
  293.0 8.8 %skip.1.base = f32[8192,128]{1,0:T(8,128)} custom-call(bf16[256,768]{1,0:T(8,128)(2,1)} %pad_maximum_fusion.kron, f32[256,1]{1,0:T(8,128)} %broadcast_in_dim_tile.4.bias, f32[8192,128]{1,0:T(8,128)} %get-tuple-element.8.latent), custom_call_target="tpu_custom_call" | custom-call | bytes 24000000 | tf_op jit(solution)/shard_map/skip/pallas_call | solution.py:505
  301.8 5.3 %all-to-all-done.3 = f32[64,40,128]{2,1,0:T(8,128)S(1)} async-done(((f32[64,40,128]{2,1,0:T(8,128)}), f32[64,40,128]{2,1,0:T(8,128)S(1)}, u32[]{:S(2)}, u32[]{:S(2)}) %all-to-all-start.3) | async-done | bytes 1310752 | tf_op jit(solution)/shard_map/all_to_all | solution.py:536
  307.0 0.0 copy-start
  307.0 1.1 copy-done
  308.2 36.7 %decode.1 = f32[64,6,128]{2,1,0:T(8,128)} custom-call(s32[64,12]{1,0:T(8,128)} %convert_bitcast_fusion.tags, f32[2560,128]{1,0:T(8,128)} %bitcast.40, f32[8192,128]{1,0:T(8,128)} %skip.1.base, bf16[384,128,256]{2,1,0:T(8,128)(2,1)} %profile.1, bf16[256,192]{1,0:T(8,128)(2,1)} %constant.46.clone.iy, bf16[768,256]{1,0:T(8,128)(2,1)} %constant.47.clone.iz, ...), custom_call_target="tpu_custom_call" | custom-call | tf_op jit(solution)/shard_map/decode/pallas_call | solution.py:537
  344.9 6.2 %all-to-all-start.4 = ((f32[64,6,128]{2,1,0:T(8,128)}), f32[64,6,128]{2,1,0:T(8,128)S(1)}, u32[]{:S(2)}, u32[]{:S(2)}) async-start(f32[64,6,128]{2,1,0:T(8,128)} %decode.1), calls=%async_computation.4 | async-start | bytes 524288 | tf_op jit(solution)/shard_map/all_to_all | solution.py:568
  351.1 0.7 fusion.11
  351.8 11.3 %all-to-all-done.4 = f32[64,6,128]{2,1,0:T(8,128)S(1)} async-done(((f32[64,6,128]{2,1,0:T(8,128)}), f32[64,6,128]{2,1,0:T(8,128)S(1)}, u32[]{:S(2)}, u32[]{:S(2)}) %all-to-all-start.4) | async-done | bytes 196640 | tf_op jit(solution)/shard_map/all_to_all | solution.py:568
  363.1 1.8 gather_fusion
  (9 shorter events, 0.1 us)
Async XLA Ops:
  5.8 35.9 %all-to-all-start = ((f32[64,24,128]{2,1,0:T(8,128)}), f32[64,24,128]{2,1,0:T(8,128)S(1)}, u32[]{:S(2)}, u32[]{:S(2)}) async-start(f32[64,24,128]{2,1,0:T(8,128)} %queries.1), calls=%async_computation | async-start | bytes 1572864 | tf_op jit(solution)/shard_map/all_to_all | solution.py:469
  41.8 6.4 %copy-start.1 = (f32[64,24,128]{2,1,0:T(8,128)}, f32[64,24,128]{2,1,0:T(8,128)S(1)}, u32[]{:S(2)}) copy-start(f32[64,24,128]{2,1,0:T(8,128)S(1)} %all-to-all-done.pos) | copy-start | bytes 2359300
  41.8 147.2 %all-to-all-start.1 = ((f32[384,32,128]{2,1,0:T(8,128)}), f32[384,32,128]{2,1,0:T(8,128)}, u32[]{:S(2)}, u32[]{:S(2)}) async-start(f32[384,32,128]{2,1,0:T(8,128)} %encode.1), calls=%async_computation.1 | async-start | bytes 12582912 | tf_op jit(solution)/shard_map/all_to_all | solution.py:470
  249.5 23.4 %copy-start.2 = (f32[32,32]{1,0:T(8,128)S(1)}, f32[32,32]{1,0:T(8,128)}, u32[]{:S(2)}) copy-start(f32[32,32]{1,0:T(8,128)} %param.28) | copy-start | bytes 12292
  266.6 6.9 %copy-start.4 = (f32[32]{0:T(128)S(1)}, f32[32]{0:T(128)}, u32[]{:S(2)}) copy-start(f32[32]{0:T(128)} %param.29) | copy-start | bytes 388
  266.6 7.7 %copy-start.3 = (f32[32,32]{1,0:T(8,128)S(1)}, f32[32,32]{1,0:T(8,128)}, u32[]{:S(2)}) copy-start(f32[32,32]{1,0:T(8,128)} %param.30) | copy-start | bytes 12292
  266.6 8.2 %copy-start.5 = (f32[32]{0:T(128)S(1)}, f32[32]{0:T(128)}, u32[]{:S(2)}) copy-start(f32[32]{0:T(128)} %param.31) | copy-start | bytes 388
  266.6 40.5 %all-to-all-start.3 = ((f32[64,40,128]{2,1,0:T(8,128)}), f32[64,40,128]{2,1,0:T(8,128)S(1)}, u32[]{:S(2)}, u32[]{:S(2)}) async-start(f32[64,40,128]{2,1,0:T(8,128)} %bitcast.41), calls=%async_computation.3 | async-start | bytes 2621440 | tf_op jit(solution)/shard_map/all_to_all | solution.py:536
  307.0 1.1 copy-start
  344.9 18.1 %all-to-all-start.4 = ((f32[64,6,128]{2,1,0:T(8,128)}), f32[64,6,128]{2,1,0:T(8,128)S(1)}, u32[]{:S(2)}, u32[]{:S(2)}) async-start(f32[64,6,128]{2,1,0:T(8,128)} %decode.1), calls=%async_computation.4 | async-start | bytes 524288 | tf_op jit(solution)/shard_map/all_to_all | solution.py:568

commit v3 on v2

--- a/solution.py
+++ b/solution.py
@@ -316,41 +316,115 @@
     return u, pltpu.roll(w, 64, 1)
 
 
-def mix_kernel(spec, weight, fx, spread, gather, ix, out):
-    step = pl.program_id(0)
+def mix_rows(spec, weight, fx, spread, gather, ix, out, pitch, row, kz, count):
     lane = lax.broadcasted_iota(jnp.int32, (64, 128), 1)
     first_plane = (lane & 32) == 0
     real_part = lane < 64
     data = jnp.concatenate(
-        [spec[pl.ds(step * 3 + n, SLABS, stride=MROWS), :] for n in range(3)], axis=1
+        [spec[pl.ds(row + n, SLABS, stride=pitch), :] for n in range(count)], axis=1
     )
     t = mm(fx[...], right3(data))
     rows = []
-    for n in range(3):
+    for n in range(count):
         u, w = planes_of(t[:, n * 128 : n * 128 + 128], first_plane)
         rows.append(u + jnp.where(real_part, w, -w))
     sh, sl = split(jnp.concatenate(rows, axis=0))
     wide = mm(jnp.concatenate([sh, sl], axis=1), spread[...])
     rows = []
-    for n in range(3):
+    for n in range(count):
         acc_re = jnp.zeros((64, 128), F32)
         acc_im = jnp.zeros((64, 128), F32)
         part = slice(n * 64, n * 64 + 64)
         for piece in range(8):
             re = slice(piece * 128, piece * 128 + 128)
             im = slice(C * C + piece * 128, C * C + piece * 128 + 128)
-            w_re = weight[n, :, re].astype(F32)
-            w_im = weight[n, :, im].astype(F32)
+            w_re = weight[kz + n, :, re].astype(F32)
+            w_im = weight[kz + n, :, im].astype(F32)
             acc_re += wide[part, re] * w_re - wide[part, im] * w_im
             acc_im += wide[part, re] * w_im + wide[part, im] * w_re
         rows.append(jnp.concatenate([acc_re, acc_im], axis=1))
     ah, al = split(jnp.concatenate(rows, axis=0))
     o = mm(jnp.concatenate([ah, al], axis=1), gather[...])
-    data = jnp.concatenate([o[n * 64 : n * 64 + 64] for n in range(3)], axis=1)
+    data = jnp.concatenate([o[n * 64 : n * 64 + 64] for n in range(count)], axis=1)
     t = mm(ix[...], right3(data))
-    for n in range(3):
+    for n in range(count):
         u, w = planes_of(t[:, n * 128 : n * 128 + 128], first_plane)
-        out[pl.ds(step * 3 + n, SLABS, stride=MROWS), :] = u + jnp.where(real_part, -w, w)
+        out[pl.ds(row + n, SLABS, stride=pitch), :] = u + jnp.where(real_part, -w, w)
+
+
+GROUPS = ((0, 16, 16), (16, 16, 16), (32, 1, 8))
+
+
+def mix_kernel(
+    message, weight_far, fx, spread, gather, ix, out,
+    spec_0, spec_1, spec_2, ready_0, ready_1, ready_2, weight,
+    send_a, recv_a, send_b, recv_b, weight_sem,
+):
+    specs, readies = (spec_0, spec_1, spec_2), (ready_0, ready_1, ready_2)
+    me = lax.axis_index("slab")
+    barrier = pltpu.get_barrier_semaphore()
+    mesh_id = pl.DeviceIdType.MESH
+
+    def greet(k, carry):
+        peer = lax.rem(me + k, SLABS)
+        pl.semaphore_signal(barrier, inc=1, device_id={"slab": peer}, device_id_type=mesh_id)
+        return carry
+
+    lax.fori_loop(1, SLABS, greet, 0)
+    fetch = pltpu.make_async_copy(weight_far, weight, weight_sem)
+    fetch.start()
+    for group, (first, count, pitch) in enumerate(GROUPS):
+        near = pl.multiple_of(me * pitch, 8)
+        far = pl.multiple_of(me * MROWS + first, 8)
+        specs[group][pl.ds(near, pitch), :] = message[pl.ds(far, pitch), :]
+    pl.semaphore_wait(barrier, SLABS - 1)
+
+    def scatter(source, target, send, recv, group, source_pitch, target_pitch, count):
+        def go(k, carry):
+            peer = lax.rem(me + lax.rem(k * 27, SLABS), SLABS)
+            theirs = pl.multiple_of(peer * source_pitch[0] + source_pitch[1], 8)
+            mine = pl.multiple_of(me * target_pitch[0] + target_pitch[1], 8)
+            pltpu.make_async_remote_copy(
+                src_ref=source.at[pl.ds(theirs, count)],
+                dst_ref=target.at[pl.ds(mine, count)],
+                send_sem=send.at[group],
+                recv_sem=recv.at[group],
+                device_id={"slab": peer},
+                device_id_type=mesh_id,
+            ).start()
+            return carry
+
+        lax.fori_loop(1, SLABS, go, 0)
+
+    def settle(ref, sem, group, count):
+        part = ref.at[pl.ds(0, (SLABS - 1) * count)]
+        pltpu.make_async_copy(part, part, sem.at[group]).wait()
+
+    for group, (first, count, pitch) in enumerate(GROUPS):
+        scatter(message, specs[group], send_a, recv_a, group, (MROWS, first), (pitch, 0), count)
+    fetch.wait()
+    for group, (first, count, pitch) in enumerate(GROUPS):
+        spec, ready = specs[group], readies[group]
+        settle(spec, recv_a, group, count)
+        if count == 1:
+            ready[...] = jnp.zeros_like(ready)
+            mix_rows(spec, weight, fx, spread, gather, ix, ready, pitch, 0, first, 1)
+        else:
+
+            def four(i, carry):
+                row = 4 * i
+                mix_rows(spec, weight, fx, spread, gather, ix, ready, pitch, row, first + row, 4)
+                return carry
+
+            lax.fori_loop(0, count // 4, four, 0)
+        scatter(ready, out, send_b, recv_b, group, (pitch, 0), (MROWS, first), count)
+        near = pl.multiple_of(me * pitch, 8)
+        far = pl.multiple_of(me * MROWS + first, 8)
+        out[pl.ds(far, pitch), :] = ready[pl.ds(near, pitch), :]
+    for group, (first, count, pitch) in enumerate(GROUPS):
+        settle(message, send_a, group, count)
+        settle(readies[group], send_b, group, count)
+        settle(out, recv_b, group, count)
 
 
 def decode_kernel(tags, inverse, base, profile, iy, iz, dw, ow, out, modes, hidden):
@@ -479,6 +553,7 @@
         cost_estimate=cost(25),
         name="profile",
     )(got_queries)
+    tags, profile = lax.optimization_barrier((tags, profile))
     skip_wide = left_table(jnp.kron(jnp.eye(8, dtype=F32), skip_weight.T))
     skip_bias_wide = jnp.tile(skip_bias, 8)[:, None]
     dec_wide = left_table(jnp.kron(jnp.eye(CAP, dtype=F32), dec_weight.T))
@@ -501,7 +576,6 @@
         compiler_params=params(),
         name="forward",
     )(tags, got_terms, forward_y, forward_z)
-    spectrum = exchange(message)
     base = pl.pallas_call(
         skip_kernel,
         out_shape=jax.ShapeDtypeStruct((LINES * C, NZ), F32),
@@ -517,23 +591,25 @@
         name="skip",
     )(skip_wide, skip_bias_wide, latent)
     weight = jnp.transpose(mode_weight.reshape(MX, MZ, 2 * C * C), (1, 0, 2))
-    mixed = pl.pallas_call(
+    vm = pl.BlockSpec(memory_space=pltpu.VMEM)
+    inverse = pl.pallas_call(
         mix_kernel,
         out_shape=jax.ShapeDtypeStruct((SLABS * MROWS, 128), F32),
-        grid=(11,),
-        in_specs=[
-            whole((SLABS * MROWS, 128)),
-            pl.BlockSpec((3, MX, 2 * C * C), lambda i: (i, 0, 0)),
-            whole((256, 192)),
-            whole((256, 2 * C * C)),
-            whole((512, 128)),
-            whole((256, 192)),
+        in_specs=[vm, pl.BlockSpec(memory_space=pl.ANY), vm, vm, vm, vm],
+        out_specs=vm,
+        scratch_shapes=[
+            *[pltpu.VMEM((SLABS * pitch, 128), F32) for _, _, pitch in GROUPS],
+            *[pltpu.VMEM((SLABS * pitch, 128), F32) for _, _, pitch in GROUPS],
+            pltpu.VMEM((MZ, MX, 2 * C * C), BF),
+            pltpu.SemaphoreType.DMA((3,)),
+            pltpu.SemaphoreType.DMA((3,)),
+            pltpu.SemaphoreType.DMA((3,)),
+            pltpu.SemaphoreType.DMA((3,)),
+            pltpu.SemaphoreType.DMA,
         ],
-        out_specs=whole((SLABS * MROWS, 128)),
-        compiler_params=params(),
+        compiler_params=params(collective_id=0, has_side_effects=True),
         name="mix",
-    )(spectrum.reshape(SLABS * MROWS, 128), weight, forward_x, spread, gather, inverse_x)
-    inverse = exchange(mixed.reshape(SLABS, MROWS, 128))
+    )(message.reshape(SLABS * MROWS, 128), weight, forward_x, spread, gather, inverse_x)
     answers = pl.pallas_call(
         decode_kernel,
         out_shape=jax.ShapeDtypeStruct((SLABS, CAP, PB), F32),
@@ -557,7 +633,7 @@
         name="decode",
     )(
         tags,
-        inverse.reshape(MY * MROWS, 128),
+        inverse,
         base,
         profile,
         inverse_y,

time: 367 us -> 335 us (0.913)
  Pallas kernels: 117 us -> 159 us
  blocking collectives: 39.9 us -> 0 us
  waiting for transfers between devices: 167 us -> 142 us
  starting transfers between devices: 31.8 us -> 25.3 us
    pallas_call x1, Pallas kernels: 17.1 us -> 59.2 us  [local(): pl.pallas_call(mix_kernel, out_shape=jax.ShapeDtypeStruct((SLABS * MROWS,...]
    all_to_all x1 -> x0, blocking collectives: 39.9 us -> none  [local(): spectrum = exchange(message)]
    all_to_all x1, waiting for transfers between devices: 140 us -> 120 us  [local(): got_terms = exchange(packed)]
    all_to_all x1 -> x0, starting transfers between devices: 6.31 us -> none  [local(): inverse = exchange(mixed.reshape(SLABS, MROWS, 128))]
    all_to_all x1 -> x0, waiting for transfers between devices: 5.25 us -> none  [local(): inverse = exchange(mixed.reshape(SLABS, MROWS, 128))]
  transfers between devices with their start and end apart: 4 -> 3, of which waited for: 4 -> 3; matrix products, arithmetic and copies ran while one was open for 2% -> 2% of each run, Pallas kernels for 10% -> 8%
where the time goes in v3:
time: 335 us; the launch traced here: 334 us
  Pallas kernels  159 us (47%)
  waiting for transfers between devices  142 us (42%)
  starting transfers between devices  25.3 us (8%)
  other arithmetic  3.91 us (1%)
  local copies, waits for them, and re-layouts  3.6 us (1%)
    all_to_all x1, waiting for transfers between devices, local(): got_terms = exchange(packed)  120 us
    pallas_call x1, Pallas kernels, local(): pl.pallas_call(mix_kernel, out_shape=jax.ShapeDtypeStruct((SLABS * MROWS,...  59.2 us
    pallas_call x1, Pallas kernels, local(): pl.pallas_call(decode_kernel, out_shape=jax.ShapeDtypeStruct((SLABS, CAP,...  36.8 us
    pallas_call x1, Pallas kernels, local(): pl.pallas_call(forward_kernel, out_shape=(jax.ShapeDtypeStruct((LINES * C...  20.2 us
    pallas_call x1, Pallas kernels, local(): pl.pallas_call(profile_kernel, out_shape=jax.ShapeDtypeStruct((SLOTS, NZ,...  15.8 us
    all_to_all x1, starting transfers between devices, local(): got_queries = exchange(queries)  13 us
    pallas_call x1, Pallas kernels, local(): pl.pallas_call(encode_kernel, out_shape=jax.ShapeDtypeStruct((SLOTS, C, N...  12.3 us
    all_to_all x1, waiting for transfers between devices, local(): returned = exchange(answers)  11.3 us
  transfers between devices with their start and end apart: 3, of which 3 were waited for; matrix products, arithmetic and copies ran while one was open for 2% of the time, Pallas kernels for 8%

profile of v3, /device:TPU:1, one launch (start us, length us, event | category | flops | bytes accessed | tf_op | source)
XLA Modules:
  0.0 333.5 jit_solution(3252392147528469635)
XLA Ops:
  0.0 1.6 routes.1.route
  1.6 4.2 %queries.1 = f32[64,24,128]{2,1,0:T(8,128)} custom-call(s32[8,384]{1,0:T(8,128)} %routes.1.route, f32[3,128,128]{2,1,0:T(8,128)} %bitcast.39), custom_call_target="tpu_custom_call" | custom-call | tf_op jit(solution)/shard_map/queries/pallas_call | solution.py:521
  5.9 13.0 %all-to-all-start = ((f32[64,24,128]{2,1,0:T(8,128)}), f32[64,24,128]{2,1,0:T(8,128)S(1)}, u32[]{:S(2)}, u32[]{:S(2)}) async-start(f32[64,24,128]{2,1,0:T(8,128)} %queries.1), calls=%async_computation | async-start | bytes 1572864 | tf_op jit(solution)/shard_map/all_to_all | solution.py:543
  18.8 12.3 %encode.1 = f32[384,32,128]{2,1,0:T(8,128)} custom-call(s32[8,384]{1,0:T(8,128)} %routes.1.route, f32[128,32,128]{2,1,0:T(8,128)} %feat.1, f32[3,128,128]{2,1,0:T(8,128)} %bitcast.40), custom_call_target="tpu_custom_call" | custom-call | bytes 24000000 | tf_op jit(solution)/shard_map/encode/pallas_call | solution.py:528
  31.1 0.0 copy-start.3
  31.1 0.0 copy-start.1
  31.1 0.0 copy-start.2
  31.1 0.0 copy-start.4
  31.1 10.6 %all-to-all-done.pos = f32[64,24,128]{2,1,0:T(8,128)S(1)} async-done(((f32[64,24,128]{2,1,0:T(8,128)}), f32[64,24,128]{2,1,0:T(8,128)S(1)}, u32[]{:S(2)}, u32[]{:S(2)}) %all-to-all-start) | async-done | bytes 786464 | tf_op jit(solution)/shard_map/all_to_all | solution.py:543
  41.8 0.0 copy-start
  41.8 6.4 %all-to-all-start.1 = ((f32[384,32,128]{2,1,0:T(8,128)}), f32[384,32,128]{2,1,0:T(8,128)}, u32[]{:S(2)}, u32[]{:S(2)}) async-start(f32[384,32,128]{2,1,0:T(8,128)} %encode.1), calls=%async_computation.1 | async-start | bytes 12582912 | tf_op jit(solution)/shard_map/all_to_all | solution.py:544
  48.2 0.0 copy-done.3
  48.2 0.1 mul.88
  48.3 0.0 copy-done.1
  48.3 0.1 copy.33
  48.3 0.0 copy-done.2
  48.3 0.1 copy.35
  48.4 0.1 mul.85
  48.5 0.1 mul.86
  48.6 0.0 copy-done.4
  48.6 0.8 broadcast_in_dim_tile.4.bias
  49.4 0.1 broadcast_multiply_fusion.1
  49.5 0.2 mul.84
  49.7 0.1 broadcast_multiply_fusion
  49.9 0.3 mul.80
  50.2 0.7 pad_maximum_fusion.2.ow
  50.9 0.8 pad_maximum_fusion.1.dw
  51.7 0.8 pad_maximum_fusion.kron
  52.5 0.0 copy-done
  52.6 15.8 %profile.1 = bf16[384,128,256]{2,1,0:T(8,128)(2,1)} custom-call(f32[64,24,128]{2,1,0:T(8,128)} %copy-done), custom_call_target="tpu_custom_call" | custom-call | bytes 50000000 | tf_op jit(solution)/shard_map/profile/pallas_call | solution.py:546
  68.4 0.6 convert_bitcast_fusion.tags
  69.0 120.0 %all-to-all-done.1.got = f32[384,32,128]{2,1,0:T(8,128)} async-done(((f32[384,32,128]{2,1,0:T(8,128)}), f32[384,32,128]{2,1,0:T(8,128)}, u32[]{:S(2)}, u32[]{:S(2)}) %all-to-all-start.1) | async-done | bytes 6291488 | tf_op jit(solution)/shard_map/all_to_all | solution.py:544
  189.0 20.2 %forward.1 = (f32[8192,128]{1,0:T(8,128)}, f32[64,40,128]{2,1,0:T(8,128)}) custom-call(s32[64,12]{1,0:T(8,128)} %convert_bitcast_fusion.tags, f32[384,32,128]{2,1,0:T(8,128)} %all-to-all-done.1.got, bf16[128,384]{1,0:T(8,128)(2,1)} %constant.40.clone.dy, bf16[768,128]{1,0:T(8,128)(2,1)} %constant.41.clone.fz), custom_call_target="tpu_custom_call" | custom-call | tf_op jit(solution)/shard_map/forward/pallas_call | solution.py:561
  209.2 8.7 %skip.1.base = f32[8192,128]{1,0:T(8,128)} custom-call(bf16[256,768]{1,0:T(8,128)(2,1)} %pad_maximum_fusion.kron, f32[256,1]{1,0:T(8,128)} %broadcast_in_dim_tile.4.bias, f32[8192,128]{1,0:T(8,128)} %get-tuple-element.11.latent), custom_call_target="tpu_custom_call" | custom-call | bytes 24000000 | tf_op jit(solution)/shard_map/skip/pallas_call | solution.py:579
  217.9 59.2 %mix.1.inverse = f32[2560,128]{1,0:T(8,128)} custom-call(f32[2560,128]{1,0:T(8,128)} %bitcast.38, bf16[33,64,2048]{2,1,0:T(8,128)(2,1)} %bitcast.37, bf16[256,192]{1,0:T(8,128)(2,1)} %constant.42.clone.fx, bf16[256,2048]{1,0:T(8,128)(2,1)} %constant.43.clone.spread, bf16[512,128]{1,0:T(8,128)(2,1)} %constant.44.clone.gather, bf16[256,192]{1,0:T(8,128)(2,1)} %constant.45.clone.ix), custom_call_target="tpu_custom_call" | custom-call | tf_op jit(solution)/shard_map/mix/pallas_call | solution.py:595
  277.0 36.8 %decode.1 = f32[64,6,128]{2,1,0:T(8,128)} custom-call(s32[64,12]{1,0:T(8,128)} %convert_bitcast_fusion.tags, f32[2560,128]{1,0:T(8,128)} %mix.1.inverse, f32[8192,128]{1,0:T(8,128)} %skip.1.base, bf16[384,128,256]{2,1,0:T(8,128)(2,1)} %profile.1, bf16[256,192]{1,0:T(8,128)(2,1)} %constant.46.clone.iy, bf16[768,256]{1,0:T(8,128)(2,1)} %constant.47.clone.iz, ...), custom_call_target="tpu_custom_call" | custom-call | tf_op jit(solution)/shard_map/decode/pallas_call | solution.py:613
  313.8 5.9 %all-to-all-start.2 = ((f32[64,6,128]{2,1,0:T(8,128)}), f32[64,6,128]{2,1,0:T(8,128)S(1)}, u32[]{:S(2)}, u32[]{:S(2)}) async-start(f32[64,6,128]{2,1,0:T(8,128)} %decode.1), calls=%async_computation.2 | async-start | bytes 524288 | tf_op jit(solution)/shard_map/all_to_all | solution.py:644
  319.7 0.7 fusion.11
  320.4 11.3 %all-to-all-done.2 = f32[64,6,128]{2,1,0:T(8,128)S(1)} async-done(((f32[64,6,128]{2,1,0:T(8,128)}), f32[64,6,128]{2,1,0:T(8,128)S(1)}, u32[]{:S(2)}, u32[]{:S(2)}) %all-to-all-start.2) | async-done | bytes 196640 | tf_op jit(solution)/shard_map/all_to_all | solution.py:644
  331.7 1.8 gather_fusion
  (9 shorter events, 0.1 us)
Async XLA Ops:
  5.9 35.9 %all-to-all-start = ((f32[64,24,128]{2,1,0:T(8,128)}), f32[64,24,128]{2,1,0:T(8,128)S(1)}, u32[]{:S(2)}, u32[]{:S(2)}) async-start(f32[64,24,128]{2,1,0:T(8,128)} %queries.1), calls=%async_computation | async-start | bytes 1572864 | tf_op jit(solution)/shard_map/all_to_all | solution.py:543
  31.1 17.0 %copy-start.3 = (f32[32]{0:T(128)S(1)}, f32[32]{0:T(128)}, u32[]{:S(2)}) copy-start(f32[32]{0:T(128)} %param.31) | copy-start | bytes 388
  31.1 17.1 %copy-start.1 = (f32[32,32]{1,0:T(8,128)S(1)}, f32[32,32]{1,0:T(8,128)}, u32[]{:S(2)}) copy-start(f32[32,32]{1,0:T(8,128)} %param.28) | copy-start | bytes 12292
  31.1 17.2 %copy-start.2 = (f32[32,32]{1,0:T(8,128)S(1)}, f32[32,32]{1,0:T(8,128)}, u32[]{:S(2)}) copy-start(f32[32,32]{1,0:T(8,128)} %param.30) | copy-start | bytes 12292
  31.1 17.4 %copy-start.4 = (f32[32]{0:T(128)S(1)}, f32[32]{0:T(128)}, u32[]{:S(2)}) copy-start(f32[32]{0:T(128)} %param.29) | copy-start | bytes 388
  41.8 10.8 %copy-start = (f32[64,24,128]{2,1,0:T(8,128)}, f32[64,24,128]{2,1,0:T(8,128)S(1)}, u32[]{:S(2)}) copy-start(f32[64,24,128]{2,1,0:T(8,128)S(1)} %all-to-all-done.pos) | copy-start | bytes 2359300
  41.8 147.2 %all-to-all-start.1 = ((f32[384,32,128]{2,1,0:T(8,128)}), f32[384,32,128]{2,1,0:T(8,128)}, u32[]{:S(2)}, u32[]{:S(2)}) async-start(f32[384,32,128]{2,1,0:T(8,128)} %encode.1), calls=%async_computation.1 | async-start | bytes 12582912 | tf_op jit(solution)/shard_map/all_to_all | solution.py:544
  313.8 17.9 %all-to-all-start.2 = ((f32[64,6,128]{2,1,0:T(8,128)}), f32[64,6,128]{2,1,0:T(8,128)S(1)}, u32[]{:S(2)}, u32[]{:S(2)}) async-start(f32[64,6,128]{2,1,0:T(8,128)} %decode.1), calls=%async_computation.2 | async-start | bytes 524288 | tf_op jit(solution)/shard_map/all_to_all | solution.py:644

commit v4 on v3

--- a/solution.py
+++ b/solution.py
@@ -176,7 +176,7 @@
         filled = jnp.sum(jnp.where(match, 1.0, 0.0), axis=0, keepdims=True)
         source = jnp.sum(jnp.where(match, number, 0.0), axis=0, keepdims=True)
         line = jnp.sum(jnp.where(match, line_c, 0.0), axis=0, keepdims=True)
-        return slot_r, filled, source.astype(jnp.int32), line.astype(jnp.int32)
+        return dest_r * 8 + before_r.astype(jnp.int32), filled, source.astype(jnp.int32), line.astype(jnp.int32)
 
     out[...] = jnp.zeros((8, SLOTS), jnp.int32)
     _, filled, source, line = one(ed[...], el[...])
@@ -302,12 +302,6 @@
             return carry
 
         lax.fori_loop(0, MY, flip, 0, unroll=4)
-
-
-def skip_kernel(kron, bias, latent, out):
-    for n in range(4):
-        rows = slice(n * 256, n * 256 + 256)
-        out[rows, :] = mm(kron[...], right3(latent[rows, :])) + bias[...]
 
 
 def planes_of(t, first_plane):
@@ -356,9 +350,9 @@
 
 
 def mix_kernel(
-    message, weight_far, fx, spread, gather, ix, out,
-    spec_0, spec_1, spec_2, ready_0, ready_1, ready_2, weight,
-    send_a, recv_a, send_b, recv_b, weight_sem,
+    message, weight_far, latent, fx, spread, gather, ix, kron, bias, out, base,
+    spec_0, spec_1, spec_2, ready_0, ready_1, ready_2, weight, field,
+    send_a, recv_a, send_b, recv_b, weight_sem, field_sem,
 ):
     specs, readies = (spec_0, spec_1, spec_2), (ready_0, ready_1, ready_2)
     me = lax.axis_index("slab")
@@ -373,6 +367,8 @@
     lax.fori_loop(1, SLABS, greet, 0)
     fetch = pltpu.make_async_copy(weight_far, weight, weight_sem)
     fetch.start()
+    bring = pltpu.make_async_copy(latent, field, field_sem.at[0])
+    bring.start()
     for group, (first, count, pitch) in enumerate(GROUPS):
         near = pl.multiple_of(me * pitch, 8)
         far = pl.multiple_of(me * MROWS + first, 8)
@@ -402,6 +398,16 @@
 
     for group, (first, count, pitch) in enumerate(GROUPS):
         scatter(message, specs[group], send_a, recv_a, group, (MROWS, first), (pitch, 0), count)
+    bring.wait()
+
+    def skip(n, carry):
+        rows = pl.ds(pl.multiple_of(n * 256, 256), 256)
+        field[rows, :] = mm(kron[...], right3(field[rows, :])) + bias[...]
+        return carry
+
+    lax.fori_loop(0, LINES * C // 256, skip, 0)
+    leave = pltpu.make_async_copy(field, base, field_sem.at[1])
+    leave.start()
     fetch.wait()
     for group, (first, count, pitch) in enumerate(GROUPS):
         spec, ready = specs[group], readies[group]
@@ -425,6 +431,7 @@
         settle(message, send_a, group, count)
         settle(readies[group], send_b, group, count)
         settle(out, recv_b, group, count)
+    leave.wait()
 
 
 def decode_kernel(tags, inverse, base, profile, iy, iz, dw, ow, out, modes, hidden):
@@ -489,7 +496,42 @@
         result = mm(ow[...], right3(act))
         for half in range(2):
             d = pair * 2 + half
-            out[d] = result[:, half * PB : half * PB + PB]
+            out[d * 8 : d * 8 + CAP, :] = result[:, half * PB : half * PB + PB]
+
+
+def reply_kernel(answers, out, send_sem, recv_sem):
+    me = lax.axis_index("slab")
+    barrier = pltpu.get_barrier_semaphore()
+    mesh_id = pl.DeviceIdType.MESH
+
+    def greet(k, carry):
+        peer = lax.rem(me + k, SLABS)
+        pl.semaphore_signal(barrier, inc=1, device_id={"slab": peer}, device_id_type=mesh_id)
+        return carry
+
+    lax.fori_loop(1, SLABS, greet, 0)
+    here = pl.multiple_of(me * 8, 8)
+    out[pl.ds(here, 8), :] = answers[pl.ds(here, 8), :]
+    pl.semaphore_wait(barrier, SLABS - 1)
+
+    def go(k, carry):
+        peer = lax.rem(me + lax.rem(k * 27, SLABS), SLABS)
+        there = pl.multiple_of(peer * 8, 8)
+        pltpu.make_async_remote_copy(
+            src_ref=answers.at[pl.ds(there, CAP)],
+            dst_ref=out.at[pl.ds(here, CAP)],
+            send_sem=send_sem,
+            recv_sem=recv_sem,
+            device_id={"slab": peer},
+            device_id_type=mesh_id,
+        ).start()
+        return carry
+
+    lax.fori_loop(1, SLABS, go, 0)
+    everything = pl.ds(0, (SLABS - 1) * CAP)
+    came, sent = out.at[everything], answers.at[everything]
+    pltpu.make_async_copy(came, came, recv_sem).wait()
+    pltpu.make_async_copy(sent, sent, send_sem).wait()
 
 
 def local(
@@ -576,43 +618,45 @@
         compiler_params=params(),
         name="forward",
     )(tags, got_terms, forward_y, forward_z)
-    base = pl.pallas_call(
-        skip_kernel,
-        out_shape=jax.ShapeDtypeStruct((LINES * C, NZ), F32),
-        grid=(8,),
-        in_specs=[
-            whole((256, 768)),
-            whole((256, 1)),
-            pl.BlockSpec((1024, NZ), lambda i: (i, 0)),
-        ],
-        out_specs=pl.BlockSpec((1024, NZ), lambda i: (i, 0)),
-        compiler_params=params(),
-        cost_estimate=cost(12),
-        name="skip",
-    )(skip_wide, skip_bias_wide, latent)
     weight = jnp.transpose(mode_weight.reshape(MX, MZ, 2 * C * C), (1, 0, 2))
     vm = pl.BlockSpec(memory_space=pltpu.VMEM)
-    inverse = pl.pallas_call(
+    far = pl.BlockSpec(memory_space=pl.ANY)
+    inverse, base = pl.pallas_call(
         mix_kernel,
-        out_shape=jax.ShapeDtypeStruct((SLABS * MROWS, 128), F32),
-        in_specs=[vm, pl.BlockSpec(memory_space=pl.ANY), vm, vm, vm, vm],
-        out_specs=vm,
+        out_shape=(
+            jax.ShapeDtypeStruct((SLABS * MROWS, 128), F32),
+            jax.ShapeDtypeStruct((LINES * C, NZ), F32),
+        ),
+        in_specs=[vm, far, far, vm, vm, vm, vm, vm, vm],
+        out_specs=(vm, far),
         scratch_shapes=[
             *[pltpu.VMEM((SLABS * pitch, 128), F32) for _, _, pitch in GROUPS],
             *[pltpu.VMEM((SLABS * pitch, 128), F32) for _, _, pitch in GROUPS],
             pltpu.VMEM((MZ, MX, 2 * C * C), BF),
+            pltpu.VMEM((LINES * C, NZ), F32),
             pltpu.SemaphoreType.DMA((3,)),
             pltpu.SemaphoreType.DMA((3,)),
             pltpu.SemaphoreType.DMA((3,)),
             pltpu.SemaphoreType.DMA((3,)),
             pltpu.SemaphoreType.DMA,
+            pltpu.SemaphoreType.DMA((2,)),
         ],
         compiler_params=params(collective_id=0, has_side_effects=True),
         name="mix",
-    )(message.reshape(SLABS * MROWS, 128), weight, forward_x, spread, gather, inverse_x)
+    )(
+        message.reshape(SLABS * MROWS, 128),
+        weight,
+        latent,
+        forward_x,
+        spread,
+        gather,
+        inverse_x,
+        skip_wide,
+        skip_bias_wide,
+    )
     answers = pl.pallas_call(
         decode_kernel,
-        out_shape=jax.ShapeDtypeStruct((SLABS, CAP, PB), F32),
+        out_shape=jax.ShapeDtypeStruct((SLABS * 8, PB), F32),
         grid=(16,),
         in_specs=[
             SMEM,
@@ -624,7 +668,7 @@
             whole((CAP * C, 3 * CAP * C)),
             whole((CAP, 3 * CAP * C)),
         ],
-        out_specs=pl.BlockSpec((4, CAP, PB), lambda i: (i, 0, 0)),
+        out_specs=pl.BlockSpec((32, PB), lambda i: (i, 0)),
         scratch_shapes=[
             pltpu.VMEM((NY * 64, 128), F32),
             pltpu.VMEM((LINES * C, NZ), F32),
@@ -641,9 +685,16 @@
         dec_wide,
         out_wide,
     )
-    returned = exchange(answers)
-    slot = route[4, 0:BLK]
-    return returned[slot // CAP, slot % CAP]
+    returned = pl.pallas_call(
+        reply_kernel,
+        out_shape=jax.ShapeDtypeStruct((SLABS * 8, PB), F32),
+        in_specs=[vm],
+        out_specs=vm,
+        scratch_shapes=[pltpu.SemaphoreType.DMA, pltpu.SemaphoreType.DMA],
+        compiler_params=params(collective_id=1, has_side_effects=True),
+        name="reply",
+    )(answers)
+    return returned[route[4, 0:BLK]]
 
 
 def solution(mesh):

time: 335 us -> 324 us (0.967)
  waiting for transfers between devices: 142 us -> 130 us
  Pallas kernels: 159 us -> 165 us
  starting transfers between devices: 25.3 us -> 19.4 us
    all_to_all x1 -> x0, waiting for transfers between devices: 11.3 us -> none  [local(): returned = exchange(answers)]
    pallas_call x3, Pallas kernels: 105 us -> 111 us  [the longest x1 59.7 us: local(): pl.pallas_call(mix_kernel, out_shape=(jax.ShapeDtypeStruct((SLABS * MROWS...]
    all_to_all x1 -> x0, starting transfers between devices: 5.9 us -> none  [local(): returned = exchange(answers)]
  transfers between devices with their start and end apart: 3 -> 2, of which waited for: 3 -> 2; matrix products, arithmetic and copies ran while one was open for 2% -> 2% of each run, Pallas kernels for 8% -> 9%
where the time goes in v4:
time: 324 us; the launch traced here: 323 us
  Pallas kernels  165 us (51%)
  waiting for transfers between devices  130 us (40%)
  starting transfers between devices  19.4 us (6%)
  local copies, waits for them, and re-layouts  3.93 us (1%)
  other arithmetic  3.91 us (1%)
    all_to_all x1, waiting for transfers between devices, local(): got_terms = exchange(packed)  119 us
    pallas_call x1, Pallas kernels, local(): pl.pallas_call(mix_kernel, out_shape=(jax.ShapeDtypeStruct((SLABS * MROWS...  59.7 us
    pallas_call x1, Pallas kernels, local(): pl.pallas_call(decode_kernel, out_shape=jax.ShapeDtypeStruct((SLABS * 8,...  36.8 us
    pallas_call x1, Pallas kernels, local(): pl.pallas_call(forward_kernel, out_shape=(jax.ShapeDtypeStruct((LINES * C...  20.4 us
    pallas_call x1, Pallas kernels, local(): pl.pallas_call(profile_kernel, out_shape=jax.ShapeDtypeStruct((SLOTS, NZ,...  15.8 us
    pallas_call x1, Pallas kernels, local(): pl.pallas_call(reply_kernel, out_shape=jax.ShapeDtypeStruct((SLABS * 8, P...  14.7 us
    all_to_all x1, starting transfers between devices, local(): got_queries = exchange(queries)  13 us
    pallas_call x1, Pallas kernels, local(): pl.pallas_call(encode_kernel, out_shape=jax.ShapeDtypeStruct((SLOTS, C, N...  12.3 us
  transfers between devices with their start and end apart: 2, of which 2 were waited for; matrix products, arithmetic and copies ran while one was open for 2% of the time, Pallas kernels for 9%

profile of v4, /device:TPU:1, one launch (start us, length us, event | category | flops | bytes accessed | tf_op | source)
XLA Modules:
  0.0 322.7 jit_solution(17226841449829874033)
XLA Ops:
  0.0 1.6 routes.1.route
  1.6 4.2 %queries.1 = f32[64,24,128]{2,1,0:T(8,128)} custom-call(s32[8,384]{1,0:T(8,128)} %routes.1.route, f32[3,128,128]{2,1,0:T(8,128)} %bitcast.25), custom_call_target="tpu_custom_call" | custom-call | tf_op jit(solution)/shard_map/queries/pallas_call | solution.py:563
  5.8 13.0 %all-to-all-start = ((f32[64,24,128]{2,1,0:T(8,128)}), f32[64,24,128]{2,1,0:T(8,128)S(1)}, u32[]{:S(2)}, u32[]{:S(2)}) async-start(f32[64,24,128]{2,1,0:T(8,128)} %queries.1), calls=%async_computation | async-start | bytes 1572864 | tf_op jit(solution)/shard_map/all_to_all | solution.py:585
  18.8 12.3 %encode.1 = f32[384,32,128]{2,1,0:T(8,128)} custom-call(s32[8,384]{1,0:T(8,128)} %routes.1.route, f32[128,32,128]{2,1,0:T(8,128)} %feat.1, f32[3,128,128]{2,1,0:T(8,128)} %bitcast.26), custom_call_target="tpu_custom_call" | custom-call | bytes 24000000 | tf_op jit(solution)/shard_map/encode/pallas_call | solution.py:570
  31.1 0.0 copy-start.3
  31.1 0.0 copy-start.1
  31.1 0.0 copy-start.2
  31.1 0.0 copy-start.4
  31.1 10.6 %all-to-all-done.pos = f32[64,24,128]{2,1,0:T(8,128)S(1)} async-done(((f32[64,24,128]{2,1,0:T(8,128)}), f32[64,24,128]{2,1,0:T(8,128)S(1)}, u32[]{:S(2)}, u32[]{:S(2)}) %all-to-all-start) | async-done | bytes 786464 | tf_op jit(solution)/shard_map/all_to_all | solution.py:585
  41.8 0.0 copy-start
  41.8 6.4 %all-to-all-start.1 = ((f32[384,32,128]{2,1,0:T(8,128)}), f32[384,32,128]{2,1,0:T(8,128)}, u32[]{:S(2)}, u32[]{:S(2)}) async-start(f32[384,32,128]{2,1,0:T(8,128)} %encode.1), calls=%async_computation.1 | async-start | bytes 12582912 | tf_op jit(solution)/shard_map/all_to_all | solution.py:586
  48.2 0.0 copy-done.3
  48.2 0.1 mul.88
  48.3 0.0 copy-done.1
  48.3 0.1 copy.31
  48.3 0.0 copy-done.2
  48.3 0.1 copy.33
  48.4 0.1 mul.85
  48.5 0.1 mul.86
  48.6 0.0 copy-done.4
  48.6 0.8 broadcast_in_dim_tile.4.bias
  49.4 0.1 broadcast_multiply_fusion.1
  49.5 0.2 mul.84
  49.7 0.1 broadcast_multiply_fusion
  49.9 0.3 mul.80
  50.2 0.7 fusion.5
  50.9 0.7 pad_maximum_fusion.2.ow
  51.6 0.8 pad_maximum_fusion.1.dw
  52.4 0.8 pad_maximum_fusion.kron
  53.2 0.0 copy-done
  53.2 15.8 %profile.1 = bf16[384,128,256]{2,1,0:T(8,128)(2,1)} custom-call(f32[64,24,128]{2,1,0:T(8,128)} %copy-done), custom_call_target="tpu_custom_call" | custom-call | bytes 50000000 | tf_op jit(solution)/shard_map/profile/pallas_call | solution.py:588
  69.0 0.6 convert_bitcast_fusion.tags
  69.6 119.3 %all-to-all-done.1.got = f32[384,32,128]{2,1,0:T(8,128)} async-done(((f32[384,32,128]{2,1,0:T(8,128)}), f32[384,32,128]{2,1,0:T(8,128)}, u32[]{:S(2)}, u32[]{:S(2)}) %all-to-all-start.1) | async-done | bytes 6291488 | tf_op jit(solution)/shard_map/all_to_all | solution.py:586
  189.0 20.4 %forward.1 = (f32[8192,128]{1,0:T(8,128)}, f32[64,40,128]{2,1,0:T(8,128)}) custom-call(s32[64,12]{1,0:T(8,128)} %convert_bitcast_fusion.tags, f32[384,32,128]{2,1,0:T(8,128)} %all-to-all-done.1.got, bf16[128,384]{1,0:T(8,128)(2,1)} %constant.20.clone.dy, bf16[768,128]{1,0:T(8,128)(2,1)} %constant.21.clone.fz), custom_call_target="tpu_custom_call" | custom-call | tf_op jit(solution)/shard_map/forward/pallas_call | solution.py:603
  209.3 59.7 %mix.1 = (f32[2560,128]{1,0:T(8,128)}, f32[8192,128]{1,0:T(8,128)}) custom-call(f32[2560,128]{1,0:T(8,128)} %bitcast.24, bf16[33,64,2048]{2,1,0:T(8,128)(2,1)} %bitcast.23, f32[8192,128]{1,0:T(8,128)} %get-tuple-element.13.latent, bf16[256,192]{1,0:T(8,128)(2,1)} %constant.22.clone.fx, bf16[256,2048]{1,0:T(8,128)(2,1)} %constant.23.clone.spread, ...), custom_call_target="tpu_custom_call" | custom-call | tf_op jit(solution)/shard_map/mix/pallas_call | solution.py:624
  269.0 36.8 %decode.1.answers = f32[512,128]{1,0:T(8,128)} custom-call(s32[64,12]{1,0:T(8,128)} %convert_bitcast_fusion.tags, f32[2560,128]{1,0:T(8,128)} %get-tuple-element.14.inverse, f32[8192,128]{1,0:T(8,128)} %get-tuple-element.15.base, bf16[384,128,256]{2,1,0:T(8,128)(2,1)} %profile.1, bf16[256,192]{1,0:T(8,128)(2,1)} %constant.26.clone.iy, ...), custom_call_target="tpu_custom_call" | custom-call | tf_op jit(solution)/shard_map/decode/pallas_call | solution.py:657
  305.8 14.7 %reply.1 = f32[512,128]{1,0:T(8,128)} custom-call(f32[512,128]{1,0:T(8,128)} %decode.1.answers), custom_call_target="tpu_custom_call" | custom-call | tf_op jit(solution)/shard_map/reply/pallas_call | solution.py:688
  320.5 2.2 gather_fusion
  (9 shorter events, 0.1 us)
Async XLA Ops:
  5.8 35.9 %all-to-all-start = ((f32[64,24,128]{2,1,0:T(8,128)}), f32[64,24,128]{2,1,0:T(8,128)S(1)}, u32[]{:S(2)}, u32[]{:S(2)}) async-start(f32[64,24,128]{2,1,0:T(8,128)} %queries.1), calls=%async_computation | async-start | bytes 1572864 | tf_op jit(solution)/shard_map/all_to_all | solution.py:585
  31.1 17.0 %copy-start.3 = (f32[32]{0:T(128)S(1)}, f32[32]{0:T(128)}, u32[]{:S(2)}) copy-start(f32[32]{0:T(128)} %param.31) | copy-start | bytes 388
  31.1 17.1 %copy-start.1 = (f32[32,32]{1,0:T(8,128)S(1)}, f32[32,32]{1,0:T(8,128)}, u32[]{:S(2)}) copy-start(f32[32,32]{1,0:T(8,128)} %param.28) | copy-start | bytes 12292
  31.1 17.2 %copy-start.2 = (f32[32,32]{1,0:T(8,128)S(1)}, f32[32,32]{1,0:T(8,128)}, u32[]{:S(2)}) copy-start(f32[32,32]{1,0:T(8,128)} %param.30) | copy-start | bytes 12292
  31.1 17.4 %copy-start.4 = (f32[32]{0:T(128)S(1)}, f32[32]{0:T(128)}, u32[]{:S(2)}) copy-start(f32[32]{0:T(128)} %param.29) | copy-start | bytes 388
  41.8 11.5 %copy-start = (f32[64,24,128]{2,1,0:T(8,128)}, f32[64,24,128]{2,1,0:T(8,128)S(1)}, u32[]{:S(2)}) copy-start(f32[64,24,128]{2,1,0:T(8,128)S(1)} %all-to-all-done.pos) | copy-start | bytes 2359300
  41.8 147.2 %all-to-all-start.1 = ((f32[384,32,128]{2,1,0:T(8,128)}), f32[384,32,128]{2,1,0:T(8,128)}, u32[]{:S(2)}, u32[]{:S(2)}) async-start(f32[384,32,128]{2,1,0:T(8,128)} %encode.1), calls=%async_computation.1 | async-start | bytes 12582912 | tf_op jit(solution)/shard_map/all_to_all | solution.py:586

commit v5 on v4

--- a/solution.py
+++ b/solution.py
@@ -234,7 +234,7 @@
         out[d, 19:24, :] = jnp.zeros((5, 128), F32)
         return carry
 
-    lax.fori_loop(0, SLABS, peer, 0)
+    lax.fori_loop(0, SLABS, peer, 0, unroll=4)
 
 
 def profile_kernel(pos, out):
@@ -293,7 +293,7 @@
             scratch[pl.ds(at, 4 * MY), :] = mm(left3(x), fz[...])
             return carry
 
-        lax.fori_loop(0, PLANES * C // 4, quad, 0, unroll=2)
+        lax.fori_loop(0, PLANES * C // 4, quad, 0, unroll=4)
 
         def flip(j, carry):
             turned = jnp.transpose(scratch[pl.ds(j, PLANES * C, stride=MY), :])
@@ -301,7 +301,7 @@
             message[j, :, 64:128] = turned[64 : 64 + MROWS]
             return carry
 
-        lax.fori_loop(0, MY, flip, 0, unroll=4)
+        lax.fori_loop(0, MY, flip, 0, unroll=8)
 
 
 def planes_of(t, first_plane):
@@ -461,7 +461,7 @@
                 )
             return carry
 
-        lax.fori_loop(0, MZ // 3, planes, 0)
+        lax.fori_loop(0, MZ // 3, planes, 0, unroll=True)
 
         def columns(i, carry):
             rows = []
@@ -479,7 +479,7 @@
                         hidden[pl.ds(at, C), :] = jax.nn.gelu(value)
             return carry
 
-        lax.fori_loop(0, NY // 8, columns, 0)
+        lax.fori_loop(0, NY // 8, columns, 0, unroll=2)
 
     for pair in range(2):
         sides = []

time: 324 us -> 318 us (0.981)
  Pallas kernels: 165 us -> 159 us
where the time goes in v5:
time: 318 us; the launch traced here: 316 us
  Pallas kernels  159 us (50%)
  waiting for transfers between devices  130 us (41%)
  starting transfers between devices  19.4 us (6%)
  local copies, waits for them, and re-layouts  3.93 us (1%)
  other arithmetic  3.91 us (1%)
    all_to_all x1, waiting for transfers between devices, local(): got_terms = exchange(packed)  119 us
    pallas_call x1, Pallas kernels, local(): pl.pallas_call(mix_kernel, out_shape=(jax.ShapeDtypeStruct((SLABS * MROWS...  59.2 us
    pallas_call x1, Pallas kernels, local(): pl.pallas_call(decode_kernel, out_shape=jax.ShapeDtypeStruct((SLABS * 8,...  33.6 us
    pallas_call x1, Pallas kernels, local(): pl.pallas_call(forward_kernel, out_shape=(jax.ShapeDtypeStruct((LINES * C...  18 us
    pallas_call x1, Pallas kernels, local(): pl.pallas_call(profile_kernel, out_shape=jax.ShapeDtypeStruct((SLOTS, NZ,...  15.8 us
    pallas_call x1, Pallas kernels, local(): pl.pallas_call(reply_kernel, out_shape=jax.ShapeDtypeStruct((SLABS * 8, P...  14.7 us
    all_to_all x1, starting transfers between devices, local(): got_queries = exchange(queries)  13 us
    pallas_call x1, Pallas kernels, local(): pl.pallas_call(encode_kernel, out_shape=jax.ShapeDtypeStruct((SLOTS, C, N...  12.3 us
  transfers between devices with their start and end apart: 2, of which 2 were waited for; matrix products, arithmetic and copies ran while one was open for 2% of the time, Pallas kernels for 9%

profile of v5, /device:TPU:1, one launch (start us, length us, event | category | flops | bytes accessed | tf_op | source)
XLA Modules:
  0.0 316.4 jit_solution(9863851026310922034)
XLA Ops:
  0.0 1.6 routes.1.route
  1.6 3.9 %queries.1 = f32[64,24,128]{2,1,0:T(8,128)} custom-call(s32[8,384]{1,0:T(8,128)} %routes.1.route, f32[3,128,128]{2,1,0:T(8,128)} %bitcast.25), custom_call_target="tpu_custom_call" | custom-call | tf_op jit(solution)/shard_map/queries/pallas_call | solution.py:563
  5.6 13.0 %all-to-all-start = ((f32[64,24,128]{2,1,0:T(8,128)}), f32[64,24,128]{2,1,0:T(8,128)S(1)}, u32[]{:S(2)}, u32[]{:S(2)}) async-start(f32[64,24,128]{2,1,0:T(8,128)} %queries.1), calls=%async_computation | async-start | bytes 1572864 | tf_op jit(solution)/shard_map/all_to_all | solution.py:585
  18.5 12.3 %encode.1 = f32[384,32,128]{2,1,0:T(8,128)} custom-call(s32[8,384]{1,0:T(8,128)} %routes.1.route, f32[128,32,128]{2,1,0:T(8,128)} %feat.1, f32[3,128,128]{2,1,0:T(8,128)} %bitcast.26), custom_call_target="tpu_custom_call" | custom-call | bytes 24000000 | tf_op jit(solution)/shard_map/encode/pallas_call | solution.py:570
  30.8 0.0 copy-start.3
  30.8 0.0 copy-start.1
  30.8 0.0 copy-start.2
  30.9 0.0 copy-start.4
  30.9 10.6 %all-to-all-done.pos = f32[64,24,128]{2,1,0:T(8,128)S(1)} async-done(((f32[64,24,128]{2,1,0:T(8,128)}), f32[64,24,128]{2,1,0:T(8,128)S(1)}, u32[]{:S(2)}, u32[]{:S(2)}) %all-to-all-start) | async-done | bytes 786464 | tf_op jit(solution)/shard_map/all_to_all | solution.py:585
  41.5 0.0 copy-start
  41.5 6.4 %all-to-all-start.1 = ((f32[384,32,128]{2,1,0:T(8,128)}), f32[384,32,128]{2,1,0:T(8,128)}, u32[]{:S(2)}, u32[]{:S(2)}) async-start(f32[384,32,128]{2,1,0:T(8,128)} %encode.1), calls=%async_computation.1 | async-start | bytes 12582912 | tf_op jit(solution)/shard_map/all_to_all | solution.py:586
  47.9 0.0 copy-done.3
  47.9 0.1 mul.88
  48.0 0.0 copy-done.1
  48.0 0.1 copy.31
  48.1 0.0 copy-done.2
  48.1 0.1 copy.33
  48.1 0.1 mul.85
  48.2 0.1 mul.86
  48.3 0.0 copy-done.4
  48.3 0.8 broadcast_in_dim_tile.4.bias
  49.1 0.1 broadcast_multiply_fusion.1
  49.2 0.2 mul.84
  49.4 0.1 broadcast_multiply_fusion
  49.6 0.3 mul.80
  49.9 0.7 fusion.5
  50.6 0.7 pad_maximum_fusion.2.ow
  51.3 0.8 pad_maximum_fusion.1.dw
  52.2 0.8 pad_maximum_fusion.kron
  52.9 0.0 copy-done
  53.0 15.8 %profile.1 = bf16[384,128,256]{2,1,0:T(8,128)(2,1)} custom-call(f32[64,24,128]{2,1,0:T(8,128)} %copy-done), custom_call_target="tpu_custom_call" | custom-call | bytes 50000000 | tf_op jit(solution)/shard_map/profile/pallas_call | solution.py:588
  68.8 0.6 convert_bitcast_fusion.tags
  69.4 119.3 %all-to-all-done.1.got = f32[384,32,128]{2,1,0:T(8,128)} async-done(((f32[384,32,128]{2,1,0:T(8,128)}), f32[384,32,128]{2,1,0:T(8,128)}, u32[]{:S(2)}, u32[]{:S(2)}) %all-to-all-start.1) | async-done | bytes 6291488 | tf_op jit(solution)/shard_map/all_to_all | solution.py:586
  188.7 18.0 %forward.1 = (f32[8192,128]{1,0:T(8,128)}, f32[64,40,128]{2,1,0:T(8,128)}) custom-call(s32[64,12]{1,0:T(8,128)} %convert_bitcast_fusion.tags, f32[384,32,128]{2,1,0:T(8,128)} %all-to-all-done.1.got, bf16[128,384]{1,0:T(8,128)(2,1)} %constant.20.clone.dy, bf16[768,128]{1,0:T(8,128)(2,1)} %constant.21.clone.fz), custom_call_target="tpu_custom_call" | custom-call | tf_op jit(solution)/shard_map/forward/pallas_call | solution.py:603
  206.7 59.2 %mix.1 = (f32[2560,128]{1,0:T(8,128)}, f32[8192,128]{1,0:T(8,128)}) custom-call(f32[2560,128]{1,0:T(8,128)} %bitcast.24, bf16[33,64,2048]{2,1,0:T(8,128)(2,1)} %bitcast.23, f32[8192,128]{1,0:T(8,128)} %get-tuple-element.13.latent, bf16[256,192]{1,0:T(8,128)(2,1)} %constant.22.clone.fx, bf16[256,2048]{1,0:T(8,128)(2,1)} %constant.23.clone.spread, ...), custom_call_target="tpu_custom_call" | custom-call | tf_op jit(solution)/shard_map/mix/pallas_call | solution.py:624
  265.9 33.6 %decode.1.answers = f32[512,128]{1,0:T(8,128)} custom-call(s32[64,12]{1,0:T(8,128)} %convert_bitcast_fusion.tags, f32[2560,128]{1,0:T(8,128)} %get-tuple-element.14.inverse, f32[8192,128]{1,0:T(8,128)} %get-tuple-element.15.base, bf16[384,128,256]{2,1,0:T(8,128)(2,1)} %profile.1, bf16[256,192]{1,0:T(8,128)(2,1)} %constant.26.clone.iy, ...), custom_call_target="tpu_custom_call" | custom-call | tf_op jit(solution)/shard_map/decode/pallas_call | solution.py:657
  299.5 14.7 %reply.1 = f32[512,128]{1,0:T(8,128)} custom-call(f32[512,128]{1,0:T(8,128)} %decode.1.answers), custom_call_target="tpu_custom_call" | custom-call | tf_op jit(solution)/shard_map/reply/pallas_call | solution.py:688
  314.2 2.2 gather_fusion
  (9 shorter events, 0.1 us)
Async XLA Ops:
  5.6 35.9 %all-to-all-start = ((f32[64,24,128]{2,1,0:T(8,128)}), f32[64,24,128]{2,1,0:T(8,128)S(1)}, u32[]{:S(2)}, u32[]{:S(2)}) async-start(f32[64,24,128]{2,1,0:T(8,128)} %queries.1), calls=%async_computation | async-start | bytes 1572864 | tf_op jit(solution)/shard_map/all_to_all | solution.py:585
  30.8 17.0 %copy-start.3 = (f32[32]{0:T(128)S(1)}, f32[32]{0:T(128)}, u32[]{:S(2)}) copy-start(f32[32]{0:T(128)} %param.31) | copy-start | bytes 388
  30.8 17.1 %copy-start.1 = (f32[32,32]{1,0:T(8,128)S(1)}, f32[32,32]{1,0:T(8,128)}, u32[]{:S(2)}) copy-start(f32[32,32]{1,0:T(8,128)} %param.28) | copy-start | bytes 12292
  30.8 17.2 %copy-start.2 = (f32[32,32]{1,0:T(8,128)S(1)}, f32[32,32]{1,0:T(8,128)}, u32[]{:S(2)}) copy-start(f32[32,32]{1,0:T(8,128)} %param.30) | copy-start | bytes 12292
  30.9 17.4 %copy-start.4 = (f32[32]{0:T(128)S(1)}, f32[32]{0:T(128)}, u32[]{:S(2)}) copy-start(f32[32]{0:T(128)} %param.29) | copy-start | bytes 388
  41.5 11.5 %copy-start = (f32[64,24,128]{2,1,0:T(8,128)}, f32[64,24,128]{2,1,0:T(8,128)S(1)}, u32[]{:S(2)}) copy-start(f32[64,24,128]{2,1,0:T(8,128)S(1)} %all-to-all-done.pos) | copy-start | bytes 2359300
  41.5 147.2 %all-to-all-start.1 = ((f32[384,32,128]{2,1,0:T(8,128)}), f32[384,32,128]{2,1,0:T(8,128)}, u32[]{:S(2)}, u32[]{:S(2)}) async-start(f32[384,32,128]{2,1,0:T(8,128)} %encode.1), calls=%async_computation.1 | async-start | bytes 12582912 | tf_op jit(solution)/shard_map/all_to_all | solution.py:586
